TPU v7x, 32 devices: a whole 2x2x4 slice. The times are simulated.
32 devices in a mesh: rep: 2 (over y), fsdp: 16 (over z, x, core).
Axes of the slice: x: 2, y: 2, z: 4, core: 2. Of those that a mesh axis runs over, the one named last changes fastest.
Arguments:
- tokens: float32 [32768, 768], P(('rep', 'fsdp')), may hold values from -6 to 6
- pre_gain: bfloat16 [768], P('fsdp'), may hold values from 0.5 to 1.5
- pre_shift: bfloat16 [768], P('fsdp'), may hold values from -2 to 2
- inward_weight: bfloat16 [768, 2304], P('fsdp'), may hold values from -0.21875 to 0.21875
- inward_bias: bfloat16 [2304], P('fsdp'), may hold values from -3 to 3
- rotary_freqs: bfloat16 [768], P('fsdp'), may hold values from 0.019897461 to 1
- outward_weight: bfloat16 [768, 768], P('fsdp'), may hold values from -0.875 to 0.875
- outward_bias: bfloat16 [768], P('fsdp'), may hold values from -2 to 2
- mlp_gain: bfloat16 [768], P('fsdp'), may hold values from 0.5 to 1.5
- mlp_shift: bfloat16 [768], P('fsdp'), may hold values from -2 to 2
- up_weight: bfloat16 [768, 3072], P('fsdp'), may hold values from -0.21875 to 0.21875
- up_bias: bfloat16 [3072], P('fsdp'), may hold values from -3 to 3
- down_weight: bfloat16 [3072, 768], P('fsdp'), may hold values from -0.109375 to 0.109375
- down_bias: bfloat16 [768], P('fsdp'), may hold values from -2 to 2
- keep_mask: int32 [32, 1024], P(('rep', 'fsdp')), may hold values 0 or 1
- kept_counts: int32 [32], P(('rep', 'fsdp')), may hold values from 1 to 1024, 26624 in all
- patch_rows: int32 [32, 1024], P(('rep', 'fsdp')), may hold values from 0 to 31
- patch_cols: int32 [32, 1024], P(('rep', 'fsdp')), may hold values from 0 to 31
- cotangent: float32 [32768, 768], P(('rep', 'fsdp')), may hold values from -6 to 6
Outputs:
- outputs: float32 [32768, 768], P(('rep', 'fsdp'))
- grad_tokens: float32 [32768, 768], P(('rep', 'fsdp'))
- grad_pre_gain: float32 [768], P('fsdp')
- grad_pre_shift: float32 [768], P('fsdp')
- grad_inward_weight: float32 [768, 2304], P('fsdp')
- grad_inward_bias: float32 [1536], P('fsdp')
- grad_value_bias: float32 [768], P('fsdp')
- grad_freqs: float32 [768], P('fsdp')
- grad_outward_weight: float32 [768, 768], P('fsdp')
- grad_outward_bias: float32 [768], P('fsdp')
- grad_mlp_gain: float32 [768], P('fsdp')
- grad_mlp_shift: float32 [768], P('fsdp')
- grad_up_weight: float32 [768, 3072], P('fsdp')
- grad_up_bias: float32 [3072], P('fsdp')
- grad_down_weight: float32 [3072, 768], P('fsdp')
- grad_down_bias: float32 [768], P('fsdp')
Inputs may be any that keep to these rules, and one draw needn't show every extreme that they name: `kept_counts`: the counts add up to 26624 and some image keeps all 1024 slots.
All inputs are finite; a program needn't handle non-finite values. No bound on the sum of `keep_mask` or of `kept_counts` on one device may be relied on, other than what follows from the above.
Results may differ from a plain program's by a relative error of at most 0.013.
Values may be sent and summed in bfloat16 or wider, within the bound.
No kernel may reach another device: no remote copies, remote signals or barrier semaphores. Data moves between devices by JAX's collectives and lax.ppermute only.
A program may use at most 192 MiB of HBM per device.

v0:
```python
from functools import partial

import jax
import jax.numpy as jnp
from jax import lax
from jax.sharding import PartitionSpec as P

HD = 64


epsilon = 1e-06
masked_score = -1e30


def layer_norm(values, gain_vec, shift_vec):
    center = values - jnp.mean(values, axis=-1, keepdims=True)
    spread = jnp.mean(center * center, axis=-1, keepdims=True)
    return center * lax.rsqrt(spread + epsilon) * gain_vec + shift_vec


def rotate(vectors, cosine, sine_part):
    half_dim = vectors.shape[-1] // 2
    first_half = vectors[..., :half_dim]
    second_half = vectors[..., half_dim:]
    return jnp.concatenate(
        [
            first_half * cosine - second_half * sine_part,
            first_half * sine_part + second_half * cosine,
        ],
        axis=-1,
    )


def rope_pair(query_raw, key_raw, freq_pairs, rows_f, cols_f):
    total_rows, heads_count, head_size = query_raw.shape
    angles = cols_f[:, None] * freq_pairs[:, 0] + rows_f[:, None] * freq_pairs[:, 1]
    angles = angles.reshape(total_rows, heads_count, head_size // 2)
    cosine = jnp.cos(angles)
    sine_part = jnp.sin(angles)
    return (rotate(query_raw, cosine, sine_part), rotate(key_raw, cosine, sine_part))


def matmul(left_op, right_op):
    return jnp.dot(left_op, right_op, preferred_element_type=jnp.float32)


def left_t(left_op, right_op):
    return lax.dot_general(
        left_op, right_op, (((0,), (0,)), ((), ())), preferred_element_type=jnp.float32
    )


def right_t(left_op, right_op):
    return lax.dot_general(
        left_op, right_op, (((1,), (1,)), ((), ())), preferred_element_type=jnp.float32
    )


def column_sum(matrix):
    return jnp.sum(matrix.astype(jnp.float32), axis=0)


def project_inputs(tokens, pre_gain, pre_shift, inward_weight, inward_bias, freq_flat, head_size):
    total_rows, width = tokens.shape
    heads_count = width // head_size
    norm_one = layer_norm(
        tokens, pre_gain.astype(jnp.float32), pre_shift.astype(jnp.float32)
    ).astype(jnp.bfloat16)
    mixed = matmul(norm_one, inward_weight) + inward_bias.astype(jnp.float32)
    query_raw = mixed[:, :width].reshape(total_rows, heads_count, head_size)
    key_raw = mixed[:, width : 2 * width].reshape(total_rows, heads_count, head_size)
    value_low = (
        mixed[:, 2 * width :].reshape(total_rows, heads_count, head_size).astype(jnp.bfloat16)
    )
    freq_pairs = freq_flat.astype(jnp.float32).reshape(-1, 2)
    return (norm_one, query_raw, key_raw, value_low, freq_pairs)


def mlp_inputs(middle, mlp_gain, mlp_shift, up_weight, up_bias):
    norm_two = layer_norm(
        middle, mlp_gain.astype(jnp.float32), mlp_shift.astype(jnp.float32)
    ).astype(jnp.bfloat16)
    hidden_up = matmul(norm_two, up_weight) + up_bias.astype(jnp.float32)
    return (norm_two, hidden_up)


def unit_place(index, blocks, groups, block_rows, group_heads):
    image_idx = index // (blocks * groups)
    remainder = index % (blocks * groups)
    return (image_idx, remainder // groups * block_rows, remainder % groups * group_heads)


def take_rows(stacked, image_idx, row_start, head_start, row_count, group_heads):
    zero_idx = jnp.zeros((), jnp.int32)
    return lax.dynamic_slice(
        stacked,
        (image_idx, row_start, head_start, zero_idx),
        (1, row_count, group_heads, stacked.shape[3]),
    )[0]


def allowed_block(key_ok, image_idx, row_start, block_rows):
    key_row = lax.dynamic_index_in_dim(key_ok, image_idx, 0, keepdims=False)
    query_pos = row_start + jnp.arange(block_rows, dtype=jnp.int32)
    key_pos = jnp.arange(key_row.shape[0], dtype=jnp.int32)
    return key_row[None, :] | (query_pos[:, None] == key_pos[None, :])


def attend_forward(query_blk, key_img, value_img, allowed):
    scale_factor = query_blk.shape[-1] ** (-0.5)
    scores = (
        jnp.einsum("qhd,khd->hqk", query_blk, key_img, preferred_element_type=jnp.float32)
        * scale_factor
    )
    scores = jnp.where(allowed[None], scores, masked_score)
    row_max = jnp.max(scores, axis=-1, keepdims=True)
    exp_scores = jnp.exp(scores - row_max)
    row_total = jnp.sum(exp_scores, axis=-1, keepdims=True)
    probability = (exp_scores / row_total).astype(jnp.bfloat16)
    attended = jnp.einsum(
        "hqk,khd->qhd", probability, value_img, preferred_element_type=jnp.float32
    ).astype(jnp.bfloat16)
    log_total = row_max[..., 0] + jnp.log(row_total[..., 0])
    return (attended, log_total)


def attend_backward(query_blk, key_img, value_img, allowed, grad_blk, log_total):
    scale_factor = query_blk.shape[-1] ** (-0.5)
    scores = (
        jnp.einsum("qhd,khd->hqk", query_blk, key_img, preferred_element_type=jnp.float32)
        * scale_factor
    )
    soft_full = jnp.where(allowed[None], jnp.exp(scores - log_total[..., None]), 0.0)
    grad_prob = jnp.einsum("qhd,khd->hqk", grad_blk, value_img, preferred_element_type=jnp.float32)
    inner = jnp.sum(soft_full * grad_prob, axis=-1, keepdims=True)
    grad_scores = (soft_full * (grad_prob - inner)).astype(jnp.bfloat16)
    grad_query = (
        jnp.einsum("hqk,khd->qhd", grad_scores, key_img, preferred_element_type=jnp.float32)
        * scale_factor
    )
    grad_key = (
        jnp.einsum("hqk,qhd->khd", grad_scores, query_blk, preferred_element_type=jnp.float32)
        * scale_factor
    )
    grad_value = jnp.einsum(
        "hqk,qhd->khd", soft_full.astype(jnp.bfloat16), grad_blk, preferred_element_type=jnp.float32
    )
    return (grad_query, grad_key, grad_value)


def local(
    tokens,
    pre_gain,
    pre_shift,
    inward_weight,
    inward_bias,
    rotary_freqs,
    outward_weight,
    outward_bias,
    mlp_gain,
    mlp_shift,
    up_weight,
    up_bias,
    down_weight,
    down_bias,
    keep_mask,
    kept_counts,
    patch_rows,
    patch_cols,
    cotangent,
):
    gathered = (
        lax.all_gather(pre_gain, "fsdp", axis=0, tiled=True),
        lax.all_gather(pre_shift, "fsdp", axis=0, tiled=True),
        lax.all_gather(inward_weight, "fsdp", axis=0, tiled=True),
        lax.all_gather(inward_bias, "fsdp", axis=0, tiled=True),
        lax.all_gather(rotary_freqs, "fsdp", axis=0, tiled=True),
        lax.all_gather(outward_weight, "fsdp", axis=0, tiled=True),
        lax.all_gather(outward_bias, "fsdp", axis=0, tiled=True),
        lax.all_gather(mlp_gain, "fsdp", axis=0, tiled=True),
        lax.all_gather(mlp_shift, "fsdp", axis=0, tiled=True),
        lax.all_gather(up_weight, "fsdp", axis=0, tiled=True),
        lax.all_gather(up_bias, "fsdp", axis=0, tiled=True),
        lax.all_gather(down_weight, "fsdp", axis=0, tiled=True),
        lax.all_gather(down_bias, "fsdp", axis=0, tiled=True),
    )
    (
        full_pre_gain,
        full_pre_shift,
        full_inward_weight,
        full_inward_bias,
        full_freqs,
        full_outward_weight,
        full_outward_bias,
        full_mlp_gain,
        full_mlp_shift,
        full_up_weight,
        full_up_bias,
        full_down_weight,
        full_down_bias,
    ) = gathered
    images_dev, slots = keep_mask.shape
    total_rows, width = tokens.shape
    head_size = HD
    heads_count = width // head_size
    slot_index = jnp.arange(slots, dtype=jnp.int32)
    valid_slot = slot_index[None, :] < kept_counts[:, None]
    key_ok = valid_slot & (keep_mask == 1)
    valid_rows = valid_slot.astype(jnp.float32).reshape(total_rows, 1)
    rows_f = patch_rows.astype(jnp.float32).reshape(-1)
    cols_f = patch_cols.astype(jnp.float32).reshape(-1)
    block_rows = min(512, slots)
    blocks = slots // block_rows
    group_heads = 4
    groups = heads_count // group_heads
    unit_ids = jnp.arange(images_dev * blocks * groups, dtype=jnp.int32)
    norm_one, query_raw, key_raw, value_low, freq_pairs = project_inputs(
        tokens,
        full_pre_gain,
        full_pre_shift,
        full_inward_weight,
        full_inward_bias,
        full_freqs,
        head_size,
    )
    query_rot, key_rot = rope_pair(query_raw, key_raw, freq_pairs, rows_f, cols_f)
    query4 = query_rot.astype(jnp.bfloat16).reshape(images_dev, slots, heads_count, head_size)
    key4 = key_rot.astype(jnp.bfloat16).reshape(images_dev, slots, heads_count, head_size)
    value4 = value_low.reshape(images_dev, slots, heads_count, head_size)

    def forward_unit(index):
        image_idx, row_start, head_start = unit_place(
            index, blocks, groups, block_rows, group_heads
        )
        query_blk = take_rows(query4, image_idx, row_start, head_start, block_rows, group_heads)
        key_img = take_rows(
            key4, image_idx, jnp.zeros((), jnp.int32), head_start, slots, group_heads
        )
        value_img = take_rows(
            value4, image_idx, jnp.zeros((), jnp.int32), head_start, slots, group_heads
        )
        return attend_forward(
            query_blk, key_img, value_img, allowed_block(key_ok, image_idx, row_start, block_rows)
        )

    attended_units, log_totals = lax.map(forward_unit, unit_ids)
    attended = (
        attended_units.reshape(images_dev, blocks, groups, block_rows, group_heads, head_size)
        .transpose(0, 1, 3, 2, 4, 5)
        .reshape(total_rows, width)
    )
    branch = matmul(attended, full_outward_weight) + full_outward_bias.astype(jnp.float32)
    middle = tokens + valid_rows * branch
    norm_two, hidden_up = mlp_inputs(
        middle, full_mlp_gain, full_mlp_shift, full_up_weight, full_up_bias
    )
    activ = jax.nn.gelu(hidden_up, approximate=False).astype(jnp.bfloat16)
    outputs = middle + valid_rows * (
        matmul(activ, full_down_weight) + full_down_bias.astype(jnp.float32)
    )
    again = (
        lax.all_gather(pre_gain, "fsdp", axis=0, tiled=True),
        lax.all_gather(pre_shift, "fsdp", axis=0, tiled=True),
        lax.all_gather(inward_weight, "fsdp", axis=0, tiled=True),
        lax.all_gather(inward_bias, "fsdp", axis=0, tiled=True),
        lax.all_gather(rotary_freqs, "fsdp", axis=0, tiled=True),
        lax.all_gather(outward_weight, "fsdp", axis=0, tiled=True),
        lax.all_gather(mlp_gain, "fsdp", axis=0, tiled=True),
        lax.all_gather(mlp_shift, "fsdp", axis=0, tiled=True),
        lax.all_gather(up_weight, "fsdp", axis=0, tiled=True),
        lax.all_gather(up_bias, "fsdp", axis=0, tiled=True),
        lax.all_gather(down_weight, "fsdp", axis=0, tiled=True),
    )
    (
        back_pre_gain,
        back_pre_shift,
        back_inward_weight,
        back_inward_bias,
        back_freqs,
        back_outward_weight,
        back_mlp_gain,
        back_mlp_shift,
        back_up_weight,
        back_up_bias,
        back_down_weight,
    ) = again
    norm_two_b, hidden_up_b = mlp_inputs(
        middle, back_mlp_gain, back_mlp_shift, back_up_weight, back_up_bias
    )
    grad_down = (valid_rows * cotangent).astype(jnp.bfloat16)
    gelu_value, gelu_back = jax.vjp(partial(jax.nn.gelu, approximate=False), hidden_up_b)
    activ_b = gelu_value.astype(jnp.bfloat16)
    grad_down_bias = column_sum(grad_down)
    grad_down_weight = left_t(activ_b, grad_down)
    grad_activ = right_t(grad_down, back_down_weight)
    grad_up = gelu_back(grad_activ)[0].astype(jnp.bfloat16)
    grad_up_bias = column_sum(grad_up)
    grad_up_weight = left_t(norm_two_b, grad_up)
    grad_norm_two = right_t(grad_up, back_up_weight)
    norm_out_two, norm_back_two = jax.vjp(
        layer_norm, middle, back_mlp_gain.astype(jnp.float32), back_mlp_shift.astype(jnp.float32)
    )
    grad_mid_norm, grad_mlp_gain, grad_mlp_shift = norm_back_two(grad_norm_two)
    grad_middle = cotangent + grad_mid_norm
    grad_branch = (valid_rows * grad_middle).astype(jnp.bfloat16)
    grad_outward_bias = column_sum(grad_branch)
    grad_outward_weight = left_t(attended, grad_branch)
    grad_attended = right_t(grad_branch, back_outward_weight).astype(jnp.bfloat16)
    grad_att4 = grad_attended.reshape(images_dev, slots, heads_count, head_size)
    norm_one_b, query_raw_b, key_raw_b, value_low_b, freq_pairs_b = project_inputs(
        tokens,
        back_pre_gain,
        back_pre_shift,
        back_inward_weight,
        back_inward_bias,
        back_freqs,
        head_size,
    )

    def rope_local(query_in, key_in, freq_in):
        return rope_pair(query_in, key_in, freq_in, rows_f, cols_f)

    rotated_b, rope_back = jax.vjp(rope_local, query_raw_b, key_raw_b, freq_pairs_b)
    query4_b = rotated_b[0].astype(jnp.bfloat16).reshape(images_dev, slots, heads_count, head_size)
    key4_b = rotated_b[1].astype(jnp.bfloat16).reshape(images_dev, slots, heads_count, head_size)
    value4_b = value_low_b.reshape(images_dev, slots, heads_count, head_size)

    def backward_unit(index):
        image_idx, row_start, head_start = unit_place(
            index, blocks, groups, block_rows, group_heads
        )
        start_zero = jnp.zeros((), jnp.int32)
        query_blk = take_rows(query4_b, image_idx, row_start, head_start, block_rows, group_heads)
        key_img = take_rows(key4_b, image_idx, start_zero, head_start, slots, group_heads)
        value_img = take_rows(value4_b, image_idx, start_zero, head_start, slots, group_heads)
        grad_blk = take_rows(grad_att4, image_idx, row_start, head_start, block_rows, group_heads)
        log_total = lax.dynamic_index_in_dim(log_totals, index, 0, keepdims=False)
        return attend_backward(
            query_blk,
            key_img,
            value_img,
            allowed_block(key_ok, image_idx, row_start, block_rows),
            grad_blk,
            log_total,
        )

    grad_q_units, grad_k_units, grad_v_units = lax.map(backward_unit, unit_ids)
    grad_query = (
        grad_q_units.reshape(images_dev, blocks, groups, block_rows, group_heads, head_size)
        .transpose(0, 1, 3, 2, 4, 5)
        .reshape(total_rows, heads_count, head_size)
    )
    grad_key = (
        jnp.sum(
            grad_k_units.reshape(images_dev, blocks, groups, slots, group_heads, head_size), axis=1
        )
        .transpose(0, 2, 1, 3, 4)
        .reshape(total_rows, heads_count, head_size)
    )
    grad_value = (
        jnp.sum(
            grad_v_units.reshape(images_dev, blocks, groups, slots, group_heads, head_size), axis=1
        )
        .transpose(0, 2, 1, 3, 4)
        .reshape(total_rows, width)
    )
    grad_query_raw, grad_key_raw, grad_freq_pairs = rope_back((grad_query, grad_key))
    grad_freqs = grad_freq_pairs.reshape(-1)
    grad_mixed = jnp.concatenate(
        [
            grad_query_raw.reshape(total_rows, width),
            grad_key_raw.reshape(total_rows, width),
            grad_value,
        ],
        axis=1,
    ).astype(jnp.bfloat16)
    mixed_bias_grad = column_sum(grad_mixed)
    grad_inward_bias = mixed_bias_grad[: 2 * width]
    grad_value_bias = mixed_bias_grad[2 * width :]
    grad_inward_weight = left_t(norm_one_b, grad_mixed)
    grad_norm_one = right_t(grad_mixed, back_inward_weight)
    norm_out_one, norm_back_one = jax.vjp(
        layer_norm, tokens, back_pre_gain.astype(jnp.float32), back_pre_shift.astype(jnp.float32)
    )
    grad_tok_norm, grad_pre_gain, grad_pre_shift = norm_back_one(grad_norm_one)
    grad_tokens = grad_middle + grad_tok_norm
    shards = (
        lax.psum_scatter(grad_pre_gain, "fsdp", scatter_dimension=0, tiled=True),
        lax.psum_scatter(grad_pre_shift, "fsdp", scatter_dimension=0, tiled=True),
        lax.psum_scatter(grad_inward_weight, "fsdp", scatter_dimension=0, tiled=True),
        lax.psum_scatter(grad_inward_bias, "fsdp", scatter_dimension=0, tiled=True),
        lax.psum_scatter(grad_value_bias, "fsdp", scatter_dimension=0, tiled=True),
        lax.psum_scatter(grad_freqs, "fsdp", scatter_dimension=0, tiled=True),
        lax.psum_scatter(grad_outward_weight, "fsdp", scatter_dimension=0, tiled=True),
        lax.psum_scatter(grad_outward_bias, "fsdp", scatter_dimension=0, tiled=True),
        lax.psum_scatter(grad_mlp_gain, "fsdp", scatter_dimension=0, tiled=True),
        lax.psum_scatter(grad_mlp_shift, "fsdp", scatter_dimension=0, tiled=True),
        lax.psum_scatter(grad_up_weight, "fsdp", scatter_dimension=0, tiled=True),
        lax.psum_scatter(grad_up_bias, "fsdp", scatter_dimension=0, tiled=True),
        lax.psum_scatter(grad_down_weight, "fsdp", scatter_dimension=0, tiled=True),
        lax.psum_scatter(grad_down_bias, "fsdp", scatter_dimension=0, tiled=True),
    )
    summed = lax.psum(
        (
            shards[0],
            shards[1],
            shards[2],
            shards[3],
            shards[4],
            shards[5],
            shards[6],
            shards[7],
            shards[8],
            shards[9],
            shards[10],
            shards[11],
            shards[12],
            shards[13],
        ),
        "rep",
    )
    (
        out_pre_gain,
        out_pre_shift,
        out_inward_weight,
        out_inward_bias,
        out_value_bias,
        out_freqs,
        out_outward_weight,
        out_outward_bias,
        out_mlp_gain,
        out_mlp_shift,
        out_up_weight,
        out_up_bias,
        out_down_weight,
        out_down_bias,
    ) = summed
    return (
        outputs,
        grad_tokens,
        out_pre_gain,
        out_pre_shift,
        out_inward_weight,
        out_inward_bias,
        out_value_bias,
        out_freqs,
        out_outward_weight,
        out_outward_bias,
        out_mlp_gain,
        out_mlp_shift,
        out_up_weight,
        out_up_bias,
        out_down_weight,
        out_down_bias,
    )


def solution(mesh):
    return jax.shard_map(
        local,
        mesh=mesh,
        in_specs=(
            P(("rep", "fsdp"), None),
            P("fsdp"),
            P("fsdp"),
            P("fsdp", None),
            P("fsdp"),
            P("fsdp"),
            P("fsdp", None),
            P("fsdp"),
            P("fsdp"),
            P("fsdp"),
            P("fsdp", None),
            P("fsdp"),
            P("fsdp", None),
            P("fsdp"),
            P(("rep", "fsdp"), None),
            P(("rep", "fsdp")),
            P(("rep", "fsdp"), None),
            P(("rep", "fsdp"), None),
            P(("rep", "fsdp"), None),
        ),
        out_specs=(
            P(("rep", "fsdp"), None),
            P(("rep", "fsdp"), None),
            P("fsdp"),
            P("fsdp"),
            P("fsdp", None),
            P("fsdp"),
            P("fsdp"),
            P("fsdp"),
            P("fsdp", None),
            P("fsdp"),
            P("fsdp"),
            P("fsdp"),
            P("fsdp", None),
            P("fsdp"),
            P("fsdp", None),
            P("fsdp"),
        ),
        check_vma=False,
    )
```

profile of v0, /device:TPU:0, one launch (start us, length us, event | category | flops | bytes accessed | tf_op | source)
XLA Modules:
  0.0 900.6 jit_solution(8082659657945657206)
XLA Ops:
  20.9 63.4 %all-reduce.28 = (bf16[768]{0:T(1024)(128)(2,1)S(1)}, bf16[2304]{0:T(1024)(128)(2,1)S(1)}, bf16[768]{0:T(1024)(128)(2,1)S(1)}, bf16[768]{0:T(1024)(128)(2,1)S(1)...) all-reduce(bf16[768]{0:T(1024)(128)(2,1)S(1)} %dynamic-update-slice, ...), channel_id=1, replica_groups=mesh['rep'=2,'fsdp'=16] {'fsdp'}, use_global_device_ids=true, to_apply=%add.9 | all-reduce | flops 10752 | bytes 43008
  100.2 6.3 convolution_add_fusion
  120.6 8.6 fusion.66
  130.8 66.8 %while.32 = (s32[]{:T(128)}, bf16[6,512,4,64]{1,3,2,0:T(8,128)(2,1)}, f32[6,4,512]{2,1,0:T(4,128)S(1)}, s32[6]{0:T(128)S(1)}, bf16[1,1024,12,64]{1,3,2,0:T(8,128...) while((s32[]{:T(128)}, ...), condition=%wide.region_5.6_spmd, body=%wide.region_2.5_spmd.sunk | while | flops 563214848 | bytes 28911056 | solution.py:246
  209.3 38.3 %multiply_convert_fusion.1 = (bf16[1024,3072]{1,0:T(8,128)(2,1)}, f32[1024,3072]{1,0:T(8,128)}, f32[1024,3072]{1,0:T(8,128)}) fusion(f32[3072]{0:T(1024)S(1)} %convert_element_type.159, bf16[768,3072]{1,0:T(8,128)(2,1)} %all-gather.9.cloned.1.call-done, f32[1024,768]{0,1:T(8,128)} %copy-done.10, f32[768]{0:T(1024)S(1)} %convert_element_type.157, ...), kind=kOutput, calls=%fused_computation.69 | convolution fusion | flops 5043388416 | bytes 39348224 | tf_op jit(solution)/shard_map/dot_general | solution.py:44
  247.6 17.8 %convert_reduce_fusion = (f32[3072]{0:T(1024)}, bf16[1024,3072]{1,0:T(8,128)(2,1)}) fusion(f32[1024,3072]{1,0:T(8,128)} %get-tuple-element.505, bf16[1024,768]{0,1:T(8,128)(2,1)S(1)} %copy-done.19, bf16[3072,768]{1,0:T(8,128)(2,1)} %all-gather.11.cloned.1.call-done, f32[1024,3072]{1,0:T(8,128)} %get-tuple-element.527, f32[3072]{0:T(1024)S(1)} %convert_element_type.159), kind=kOutput, calls=%fused_computation.67 | convolution fusion | flops 4885312512 | bytes 37773312 | tf_op jit(solution)/shard_map/dot_general | solution.py:54
  265.4 10.4 %fusion.82 = (f32[768]{0:T(1024)}, f32[1024,768]{1,0:T(8,128)}) fusion(bf16[1024,3072]{1,0:T(8,128)(2,1)} %get-tuple-element.533, bf16[768,3072]{1,0:T(8,128)(2,1)} %all-gather.9.cloned.1.call-done), kind=kOutput, calls=%fused_computation.155 | convolution fusion | flops 4832623616 | bytes 14158848 | tf_op jit(solution)/shard_map/dot_general | solution.py:54
  293.3 166.3 %while.33 = (s32[]{:T(128)}, f32[6,512,4,64]{1,3,2,0:T(8,128)}, f32[6,1024,4,64]{1,3,2,0:T(8,128)}, f32[6,1024,4,64]{1,3,2,0:T(8,128)}, s32[6]{0:T(128)S(1)}, /*...) while((s32[]{:T(128)}, f32[6,512,4,64]{1,3,2,0:T(8,128)}, ...), condition=%wide.region_12.13_spmd, body=%wide.region_10.12_spmd.sunk | while | flops 1375074816 | bytes 95490112 | solution.py:347
  294.8 5.5 fusion.136
  302.8 7.2 multiply_reduce_fusion.10
  322.7 5.5 fusion.136
  330.6 7.0 multiply_reduce_fusion.10
  350.3 5.5 fusion.136
  358.2 7.0 multiply_reduce_fusion.10
  378.0 5.5 fusion.136
  385.9 7.0 multiply_reduce_fusion.10
  413.5 7.0 multiply_reduce_fusion.10
  433.2 5.5 fusion.136
  441.1 7.0 multiply_reduce_fusion.10
  478.8 11.9 %multiply_add_fusion.2 = (f32[1024,12,32]{0,2,1:T(8,128)S(1)}, f32[1024,12,32]{0,2,1:T(8,128)S(1)}, f32[1024,12,32]{0,2,1:T(8,128)S(1)}, f32[1024,12,32]{0,2,1:T(8,128)S(1)}) fusion(f32[1024,12,64]{0,2,1:T(8,128)} %bitcast.179, f32[1024,12,64]{0,2,1:T(8,128)} %reshape.434, f32[1024,12,64]{0,2,1:T(8,128)} %bitcast.178, f32[1024,12,64]{0,2,1:T(8,128)S(1)} %bitcast.176, ...), kind=kLoop, calls=%fused_computation.113 | loop fusion | flops 12582912 | bytes 18885632 | tf_op jit(solution)/shard_map/transpose(jvp())/add_any | solution.py:38
  493.2 6.1 multiply_reduce_fusion.8
  502.2 6.9 fusion.72
  509.8 10.8 %fusion.74 = f32[768,3072]{1,0:T(8,128)} fusion(bf16[1024,3072]{1,0:T(8,128)(2,1)} %get-tuple-element.533, f32[1024,768]{0,1:T(8,128)} %copy-done.10, f32[768]{0:T(1024)S(1)} %copy-done.48, f32[768]{0:T(1024)S(1)} %convert_element_type.156, f32[1024]{0:T(1024)S(1)} %fusion.70, f32[1024]{0:T(1024)S(1)} %broadcast_multiply_fusion), kind=kOutput, calls=%fused_computation.148 | convolution fusion | flops 4835770368 | bytes 18888704 | tf_op jit(solution)/shard_map/dot_general | solution.py:48
  520.7 10.5 %fusion.84 = f32[3072,768]{1,0:T(8,128)} fusion(bf16[1024,3072]{1,0:T(8,128)(2,1)} %get-tuple-element.504, bf16[1024,768]{0,1:T(8,128)(2,1)} %get-tuple-element.499), kind=kOutput, calls=%fused_computation.157 | convolution fusion | flops 4831838208 | bytes 17301504 | tf_op jit(solution)/shard_map/dot_general | solution.py:48
  536.4 9.8 %fusion.81 = (f32[768]{0:T(1024)S(1)}, f32[1024,768]{1,0:T(8,128)}) fusion(bf16[768,2304]{1,0:T(8,128)(2,1)} %all-gather.5.cloned.1.call-done, bf16[1024,768]{0,1:T(8,128)(2,1)} %bitcast.193, bf16[1024,768]{0,1:T(8,128)(2,1)} %bitcast.191, bf16[1024,768]{0,1:T(8,128)(2,1)} %bitcast.188), kind=kOutput, calls=%fused_computation.154 | convolution fusion | flops 3638820096 | bytes 11406336 | tf_op jit(solution)/shard_map/dot_general | solution.py:54
  554.0 59.5 %all-reduce.25 = (f32[768]{0:T(1024)S(1)}, f32[768]{0:T(1024)S(1)}, f32[1536]{0:T(1024)S(1)}, f32[768]{0:T(1024)S(1)}, f32[768]{0:T(1024)S(1)}, /*index=5*/f32[7...) all-reduce(f32[768]{0:T(1024)S(1)} %get-tuple-element.419, ...), channel_id=2, replica_groups=mesh['rep'=2,'fsdp'=16] {'fsdp'}, use_global_device_ids=true, to_apply=%region_18.19.clone | all-reduce | flops 10752 | bytes 86016
  614.1 7.7 add_add_fusion.2
  625.7 86.3 %reduce-scatter.9.cloned.1.call-done = f32[48,3072]{1,0:T(8,128)} async-done(((f32[768,3072]{1,0:T(8,128)}), f32[48,3072]{1,0:T(8,128)}) %reduce-scatter.9.cloned.1.call-update) | async-done | bytes 589840 | tf_op jit(solution)/shard_map/reduce_scatter | solution.py:398
  712.0 115.8 %reduce-scatter.11.cloned.1.call-done = f32[192,768]{1,0:T(8,128)} async-done(((f32[3072,768]{1,0:T(8,128)}), f32[192,768]{1,0:T(8,128)}) %reduce-scatter.11.cloned.1.call-update) | async-done | bytes 589840 | tf_op jit(solution)/shard_map/reduce_scatter | solution.py:400
  827.8 9.8 %multiply_add_fusion = f32[1024,768]{0,1:T(8,128)} fusion(f32[1024,768]{0,1:T(8,128)S(1)} %copy-done.12, bf16[1024,3072]{1,0:T(8,128)(2,1)} %get-tuple-element.504, bf16[3072,768]{1,0:T(8,128)(2,1)} %all-gather.11.cloned.1.call-done, f32[768]{0:T(1024)S(1)} %convert_element_type.161, f32[1024]{0:T(1024)S(1)} %copy-done.34), kind=kOutput, calls=%fused_computation.102 | convolution fusion | flops 4834197504 | bytes 17308672 | tf_op jit(solution)/shard_map/dot_general | solution.py:44
  841.3 5.7 all-reduce.26
  847.0 39.6 %all-reduce.31.cloned.1.call-done = (f32[48,2304]{1,0:T(8,128)}, f32[48,768]{1,0:T(8,128)}, f32[48,3072]{1,0:T(8,128)}, f32[192,768]{1,0:T(8,128)}) async-done(((f32[48,2304]{1,0:T(8,128)}, f32[48,768]{1,0:T(8,128)}, f32[48,3072]{1,0:T(8,128)}, f32[192,768]{1,0:T(8,128)}), (f32[48,2304]{1,0:T(8,128)}, f32[48,768]{1,0:T(8,128)}, f32[48,3072]{1,0:T(8,128)}, ...) | async-done | bytes 1769488 | tf_op jit(solution)/shard_map/psum | solution.py:403
  (370 shorter events, 265.4 us)
Async XLA Ops:
  7.2 93.0 %all-gather.5.cloned.1.call-start = ((), (), s32[]{:S(2)}) async-start(), calls=%async_computation.4 | async-start | bytes 3760128 | tf_op jit(solution)/shard_map/all_gather | solution.py:175
  7.9 195.8 %all-gather.7.cloned.1.call-start = ((), (), s32[]{:S(2)}) async-start(), calls=%async_computation.5 | async-start | bytes 1253376 | tf_op jit(solution)/shard_map/all_gather | solution.py:178
  8.7 200.6 %all-gather.9.cloned.1.call-start = ((), (), s32[]{:S(2)}) async-start(), calls=%async_computation.6 | async-start | bytes 5013504 | tf_op jit(solution)/shard_map/all_gather | solution.py:182
  9.4 238.2 %all-gather.11.cloned.1.call-start = ((), (), s32[]{:S(2)}) async-start(), calls=%async_computation.7 | async-start | bytes 5013504 | tf_op jit(solution)/shard_map/all_gather | solution.py:184
  10.0 615.7 %reduce-scatter.7.cloned.1.call-start = ((), (), s32[]{:S(2)}) async-start(), calls=%async_computation.9 | async-start | bytes 2506752 | tf_op jit(solution)/shard_map/reduce_scatter | solution.py:394
  84.3 15.9 %copy-start.30 = (f32[768]{0:T(1024)}, f32[768]{0:T(1024)S(1)}, u32[]{:S(2)}) copy-start(f32[768]{0:T(1024)S(1)} %convert_element_type.148) | copy-start | bytes 9220
  84.4 15.9 %copy-start.45 = (f32[768]{0:T(1024)}, f32[768]{0:T(1024)S(1)}, u32[]{:S(2)}) copy-start(f32[768]{0:T(1024)S(1)} %convert_element_type.149) | copy-start | bytes 9220
  86.9 13.3 %copy-start = (f32[1024,768]{0,1:T(8,128)}, f32[1024,768]{0,1:T(8,128)S(1)}, u32[]{:S(2)}) copy-start(f32[1024,768]{0,1:T(8,128)S(1)} %copy.91) | copy-start | bytes 9437188
  90.2 10.0 %copy-start.24 = (f32[1024]{0:T(1024)}, f32[1024]{0:T(1024)S(1)}, u32[]{:S(2)}) copy-start(f32[1024]{0:T(1024)S(1)} %broadcast_multiply_fusion.1) | copy-start | bytes 12292
  91.2 9.0 %copy-start.37 = (f32[1024]{0:T(1024)}, f32[1024]{0:T(1024)S(1)}, u32[]{:S(2)}) copy-start(f32[1024]{0:T(1024)S(1)} %fusion.69) | copy-start | bytes 12292
  91.7 28.9 %copy-start.20 = (f32[12,32]{1,0:T(8,128)}, f32[12,32]{1,0:T(8,128)S(1)}, u32[]{:S(2)}) copy-start(f32[12,32]{1,0:T(8,128)S(1)} %mul.427) | copy-start | bytes 4612
  91.8 28.8 %copy-start.22 = (f32[12,32]{1,0:T(8,128)}, f32[12,32]{1,0:T(8,128)S(1)}, u32[]{:S(2)}) copy-start(f32[12,32]{1,0:T(8,128)S(1)} %mul.432) | copy-start | bytes 4612
  91.8 28.8 %copy-start.26 = (f32[1,1024]{1,0:T(1,128)}, f32[1,1024]{1,0:T(1,128)S(1)}, u32[]{:S(2)}) copy-start(f32[1,1024]{1,0:T(1,128)S(1)} %convert_element_type.153) | copy-start | bytes 12292
  91.8 28.8 %copy-start.28 = (f32[1,1024]{1,0:T(1,128)}, f32[1,1024]{1,0:T(1,128)S(1)}, u32[]{:S(2)}) copy-start(f32[1,1024]{1,0:T(1,128)S(1)} %convert_element_type.154) | copy-start | bytes 12292
  92.5 191.4 %copy-start.33 = (f32[1024]{0:T(1024)}, f32[1024]{0:T(1024)S(1)}, u32[]{:S(2)}) copy-start(f32[1024]{0:T(1024)S(1)} %fusion.68) | copy-start | bytes 12292
  92.6 116.7 %copy-start.47 = (f32[768]{0:T(1024)}, f32[768]{0:T(1024)S(1)}, u32[]{:S(2)}) copy-start(f32[768]{0:T(1024)S(1)} %convert_element_type.157) | copy-start | bytes 9220
  113.3 7.3 copy-start.7
  209.3 38.3 %copy-start.19 = (bf16[1024,768]{0,1:T(8,128)(2,1)S(1)}, bf16[1024,768]{0,1:T(8,128)(2,1)}, u32[]{:S(2)}) copy-start(bf16[1024,768]{0,1:T(8,128)(2,1)} %get-tuple-element.499) | copy-start | bytes 4718596
  289.3 336.4 %reduce-scatter.5.cloned.1.call-start = ((), (), s32[]{:S(2)}) async-start(), calls=%async_computation.8 | async-start | bytes 7520256 | tf_op jit(solution)/shard_map/reduce_scatter | solution.py:390
  302.7 7.2 slice-start
  302.7 7.2 slice-start.1
  330.5 7.0 slice-start
  491.0 8.6 copy-start.15
  493.2 7.6 copy-start.38
  493.2 7.6 copy-start.46
  509.1 202.9 %reduce-scatter.9.cloned.1.call-start = ((), (), s32[]{:S(2)}) async-start(), calls=%async_computation.10 | async-start | bytes 10027008 | tf_op jit(solution)/shard_map/reduce_scatter | solution.py:398
  520.6 307.1 %reduce-scatter.11.cloned.1.call-start = ((), (), s32[]{:S(2)}) async-start(), calls=%async_computation.11 | async-start | bytes 10027008 | tf_op jit(solution)/shard_map/reduce_scatter | solution.py:400
  531.2 355.4 %all-reduce.31.cloned.1.call-start = ((), (), s32[]{:S(2)}) async-start(), calls=%async_computation.12 | async-start | bytes 3538944 | tf_op jit(solution)/shard_map/psum | solution.py:403
  535.9 10.3 %copy-start.32 = (f32[2304]{0:T(1024)}, f32[2304]{0:T(1024)S(1)}, u32[]{:S(2)}) copy-start(f32[2304]{0:T(1024)S(1)} %convert_reduce_fusion.1) | copy-start | bytes 27652
  552.7 61.4 %copy-start.40 = (f32[1024]{0:T(1024)S(1)}, f32[1024]{0:T(1024)}, u32[]{:S(2)}) copy-start(f32[1024]{0:T(1024)} %copy-done.39) | copy-start | bytes 12292
  621.9 206.0 %copy-start.12 = (f32[1024,768]{0,1:T(8,128)S(1)}, f32[1024,768]{0,1:T(8,128)}, u32[]{:S(2)}) copy-start(f32[1024,768]{0,1:T(8,128)} %copy-done.10) | copy-start | bytes 9437188
  621.9 206.0 %copy-start.34 = (f32[1024]{0:T(1024)S(1)}, f32[1024]{0:T(1024)}, u32[]{:S(2)}) copy-start(f32[1024]{0:T(1024)} %copy-done.33) | copy-start | bytes 12292
  (44 other events, 160.6 us)
Sparse Core Ops, SparseCore 0:
  10.3 49.8 all-gather.4
  62.5 37.2 all-gather.6
  102.1 52.1 all-gather.8
  156.5 51.9 all-gather.10
  289.4 59.9 reduce-scatter.6
  509.2 87.7 reduce-scatter.4
  601.1 110.8 reduce-scatter.8
  716.7 111.0 reduce-scatter.10
  830.3 56.2 all-reduce.30
where the time goes:
time: 911 us; the launch traced here: 901 us
  matrix products  302 us (33%)
  waiting for transfers between devices  244 us (27%)
  blocking collectives  129 us (14%)
  other arithmetic  101 us (11%)
  local copies, waits for them, and re-layouts  83.9 us (9%)
  loops' own time  21.2 us (2%)
  between operations  19.4 us (2%)
    unnamed x2, blocking collectives  123 us
    reduce_scatter x1, waiting for transfers between devices, local(): lax.psum_scatter(grad_down_weight, 'fsdp', scatter_dimension=0, tiled=True)  116 us
    reduce_scatter x1, waiting for transfers between devices, local(): lax.psum_scatter(grad_up_weight, 'fsdp', scatter_dimension=0, tiled=True)  86.3 us
    dot_general x4, matrix products, matmul(): return jnp.dot(left_op, right_op, preferred_element_type=jnp.float32)  57.9 us
    unnamed x146, local copies, waits for them, and re-layouts  42.7 us
    dot_general x6, matrix products, attend_backward(): jnp.einsum('qhd,khd->hqk', grad_blk, value_img, preferred_element_type=jn...  42 us
    dot_general x4, matrix products, right_t(): lax.dot_general(left_op, right_op, (((1,), (1,)), ((), ())), preferred_el...  41.9 us
    psum x1, waiting for transfers between devices, local(): lax.psum((shards[0], shards[1], shards[2], shards[3], shards[4], shards[5...  39.6 us
  transfers between devices with their start and end apart: 9, of which 3 were waited for; matrix products, arithmetic and copies ran while one was open for 48% of the time, Pallas kernels for 0%

commit v1 on v0

v1 whole, which is shorter than its diff:
```python
import functools
import math

import jax
import jax.numpy as jnp
from jax import lax
from jax.experimental import pallas as pl
from jax.experimental.pallas import tpu as pltpu
from jax.sharding import PartitionSpec as P

HD = 64
EPS = 1e-06
NEG = -1e30
F32 = jnp.float32
BF16 = jnp.bfloat16
GH = 4
GW = GH * HD
HALF = GW // 2
VMEM_CAP = 63 * 2**20


def dims(lhs, rhs, lhs_axis, rhs_axis):
    return lax.dot_general(
        lhs, rhs, (((lhs_axis,), (rhs_axis,)), ((), ())), preferred_element_type=F32
    )


def nn(lhs, rhs):
    return dims(lhs, rhs, 1, 0)


def nt(lhs, rhs):
    return dims(lhs, rhs, 1, 1)


def tn(lhs, rhs):
    return dims(lhs, rhs, 0, 0)


def params(grid, vmem=VMEM_CAP):
    return pltpu.CompilerParams(
        dimension_semantics=("arbitrary",) * len(grid), vmem_limit_bytes=vmem
    )


def whole(shape):
    return pl.BlockSpec(shape, lambda *idx: (0,) * len(shape))


ANY = pl.BlockSpec(memory_space=pl.ANY)
SMEM = pl.BlockSpec(memory_space=pltpu.SMEM)


def cost(flops, bytes_moved, transcendental=0):
    return pl.CostEstimate(
        flops=int(flops), bytes_accessed=int(bytes_moved), transcendentals=int(transcendental)
    )


def group_perm(transposed):
    row = lax.broadcasted_iota(jnp.int32, (GW, GW), 0)
    col = lax.broadcasted_iota(jnp.int32, (GW, GW), 1)
    packed, natural = (row, col) if transposed else (col, row)
    half = packed // HALF
    head = (packed % HALF) // (HD // 2)
    source = head * HD + half * (HD // 2) + packed % (HD // 2)
    return jnp.where(source == natural, 1.0, 0.0).astype(BF16)


def packed_head_mask(head):
    lane = lax.broadcasted_iota(jnp.int32, (1, GW), 1)
    return (lane % HALF) // (HD // 2) == head


def natural_head_mask(head):
    lane = lax.broadcasted_iota(jnp.int32, (1, GW), 1)
    return lane // HD == head


def normalize(values):
    center = values - jnp.mean(values, axis=-1, keepdims=True)
    spread = jnp.mean(center * center, axis=-1, keepdims=True)
    inverse = lax.rsqrt(spread + EPS)
    return center * inverse, inverse


def load_pieces(table, sources, target, sem):
    copies = []
    slots = table.shape[0] // 2
    for source in sources:
        rows, width = source.shape[-2:]
        for one in range(source.shape[0]):
            for two in range(source.shape[1]):
                number = len(copies)
                row = pl.multiple_of(table[number] * rows, rows)
                col = pl.multiple_of(table[slots + number] * width, width)
                copies.append(
                    pltpu.make_async_copy(
                        source.at[one, two], target.at[pl.ds(row, rows), pl.ds(col, width)], sem.at[number]
                    )
                )
    return copies


def piece_count(sources):
    return sum(s.shape[0] * s.shape[1] for s in sources)


def prologue_kernel(x_ref, gain_ref, shift_ref, fc_ref, fr_ref, col_ref, row_ref, n1_ref, cos_ref, sin_ref):
    xhat, _ = normalize(x_ref[...])
    n1_ref[...] = (xhat * gain_ref[...] + shift_ref[...]).astype(BF16)
    angle = col_ref[...] * fc_ref[...] + row_ref[...] * fr_ref[...]
    cosine, sine = cos_sin(angle)
    cos_ref[...] = cosine
    sin_ref[...] = sine


QUARTER = (1.5703125, 4.837512969970703125e-4, 7.549789948768648e-8)


def cos_sin(angle):
    turns = jnp.floor(angle * 0.6366197723675814 + 0.5)
    r = ((angle - turns * QUARTER[0]) - turns * QUARTER[1]) - turns * QUARTER[2]
    r2 = r * r
    s = r + r * r2 * (-1.6666654611e-1 + r2 * (8.3321608736e-3 - 1.9515295891e-4 * r2))
    c = 1.0 - 0.5 * r2 + r2 * r2 * (4.166664568298827e-2 + r2 * (-1.388731625493765e-3 + 2.443315711809948e-5 * r2))
    quad = turns.astype(jnp.int32)
    odd = (quad & 1) == 1
    cosine = jnp.where(odd, s, c)
    sine = jnp.where(odd, c, s)
    cosine = jnp.where(((quad + 1) & 2) == 2, -cosine, cosine)
    sine = jnp.where((quad & 2) == 2, -sine, sine)
    return cosine, sine


def prologue(x, gain, shift, fc, fr, cols, rows, rb=256):
    total, width = x.shape
    pairs = width // 2
    grid = (total // rb,)
    blk = lambda w: pl.BlockSpec((rb, w), lambda i: (i, 0))
    return pl.pallas_call(
        prologue_kernel,
        grid=grid,
        in_specs=[blk(width), whole((1, width)), whole((1, width)), whole((1, pairs)), whole((1, pairs)), blk(1), blk(1)],
        out_specs=[blk(width), blk(pairs), blk(pairs)],
        out_shape=[
            jax.ShapeDtypeStruct((total, width), BF16),
            jax.ShapeDtypeStruct((total, pairs), F32),
            jax.ShapeDtypeStruct((total, pairs), F32),
        ],
        compiler_params=params(grid),
        cost_estimate=cost(total * width * 40, total * width * 10),
        name="prologue",
    )(x, gain, shift, fc, fr, cols, rows)


def qkv_kernel(g0, npieces, table, n1_ref, bias_ref, cos_ref, sin_ref, *rest):
    pieces = rest[:npieces]
    q_ref, k_ref, v_ref, w, wp, bp, sem = rest[npieces:]
    width = n1_ref.shape[1]
    groups = w.shape[1] // (3 * GW)

    @pl.when(pl.program_id(0) == 0)
    def _():
        copies = load_pieces(table, pieces, w, sem)
        for copy in copies:
            copy.start()
        perm = group_perm(False)
        for copy in copies:
            copy.wait()
        for g in range(groups):
            for part in range(2):
                packed = pl.ds((g * 2 + part) * GW, GW)
                wp[:, packed] = nn(w[:, pl.ds((g * 3 + part) * GW, GW)], perm).astype(BF16)
                natural = pl.ds(part * width + (g0 + g) * GW, GW)
                spread = jnp.broadcast_to(bias_ref[:, natural].astype(BF16), (16, GW))
                bp[:, packed] = nn(spread, perm)[:8]

    n1 = n1_ref[...]
    for g in range(groups):
        cosine = cos_ref[:, pl.ds((g0 + g) * HALF, HALF)]
        sine = sin_ref[:, pl.ds((g0 + g) * HALF, HALF)]
        for part, out, scale in ((0, q_ref, HD**-0.5), (1, k_ref, 1.0)):
            packed = pl.ds((g * 2 + part) * GW, GW)
            mixed = nn(n1, wp[:, packed]) + bp[0:1, packed]
            a, b = mixed[:, :HALF], mixed[:, HALF:]
            first = a * cosine - b * sine
            second = a * sine + b * cosine
            if scale != 1.0:
                first = first * scale
                second = second * scale
            out[:, pl.ds(g * GW, HALF)] = first.astype(BF16)
            out[:, pl.ds(g * GW + HALF, HALF)] = second.astype(BF16)
        bias = bias_ref[:, pl.ds(2 * width + (g0 + g) * GW, GW)]
        v_ref[:, pl.ds(g * GW, GW)] = (nn(n1, w[:, pl.ds((g * 3 + 2) * GW, GW)]) + bias).astype(BF16)


def qkv(g0, groups, table, n1, bias, cosine, sine, pieces, rb=256):
    total, width = n1.shape
    pairs = width // 2
    grid = (total // rb,)
    blk = lambda w: pl.BlockSpec((rb, w), lambda i: (i, 0))
    out = jax.ShapeDtypeStruct((total, groups * GW), BF16)
    copies = piece_count(pieces)
    return pl.pallas_call(
        functools.partial(qkv_kernel, g0, len(pieces)),
        grid=grid,
        in_specs=[SMEM, blk(width), whole((1, 3 * width)), blk(pairs), blk(pairs)] + [ANY] * len(pieces),
        out_specs=[blk(groups * GW)] * 3,
        out_shape=[out] * 3,
        scratch_shapes=[
            pltpu.VMEM((width, 3 * groups * GW), BF16),
            pltpu.VMEM((width, 2 * groups * GW), BF16),
            pltpu.VMEM((8, 2 * groups * GW), F32),
            pltpu.SemaphoreType.DMA((copies,)),
        ],
        compiler_params=params(grid),
        cost_estimate=cost(total * width * groups * GW * 6, total * width * 8 + width * groups * GW * 6),
        name="qkv",
    )(table, n1, bias, cosine, sine, *pieces)


def attend_kernel(q_ref, k_ref, v_ref, kb_ref, att_ref, lse_ref, mask):
    g, r = pl.program_id(0), pl.program_id(1)
    rb, keys = q_ref.shape[0], k_ref.shape[0]
    here = pl.ds(pl.multiple_of(r * rb, rb), rb)

    @pl.when(g == 0)
    def _():
        row = lax.broadcasted_iota(jnp.int32, (rb, keys), 0) + r * rb
        col = lax.broadcasted_iota(jnp.int32, (rb, keys), 1)
        mask[here, :] = jnp.where(row == col, 0.0, jnp.broadcast_to(kb_ref[...], (rb, keys)))

    q = q_ref[...]
    k = k_ref[...]
    v = v_ref[...]
    total = jnp.zeros((rb, GW), F32)
    lane = lax.broadcasted_iota(jnp.int32, (rb, 128), 1)
    logs = jnp.zeros((rb, 128), F32)
    for h in range(GH):
        qm = jnp.where(packed_head_mask(h), q, jnp.zeros_like(q))
        scores = nt(qm, k) + mask[here, :]
        top = jnp.max(scores, axis=-1, keepdims=True)
        weight = jnp.exp(scores - top)
        norm = jnp.sum(weight, axis=-1, keepdims=True)
        vm = jnp.where(natural_head_mask(h), v, jnp.zeros_like(v))
        total = total + nn(weight.astype(BF16), vm) * (1.0 / norm)
        logs = jnp.where(lane == h, top + jnp.log(norm), logs)
    att_ref[...] = total.astype(BF16)
    lse_ref[...] = jnp.transpose(logs)[:8, :]


def attend(q, k, v, kb, rb=256):
    total, width = q.shape
    groups = width // GW
    grid = (groups, total // rb)
    return pl.pallas_call(
        attend_kernel,
        grid=grid,
        in_specs=[
            pl.BlockSpec((rb, GW), lambda g, r: (r, g)),
            pl.BlockSpec((total, GW), lambda g, r: (0, g)),
            pl.BlockSpec((total, GW), lambda g, r: (0, g)),
            whole((1, total)),
        ],
        out_specs=[
            pl.BlockSpec((rb, GW), lambda g, r: (r, g)),
            pl.BlockSpec((None, 8, rb), lambda g, r: (g, 0, r)),
        ],
        out_shape=[
            jax.ShapeDtypeStruct((total, width), BF16),
            jax.ShapeDtypeStruct((groups, 8, total), F32),
        ],
        scratch_shapes=[pltpu.VMEM((total, total), F32)],
        compiler_params=params(grid),
        cost_estimate=cost(total * total * width * 16, total * width * 8, total * total * 12),
        name="attend",
    )(q, k, v, kb)


PHI_SCALE = 0.3989422804014327
TAIL_SCALE = 0.44 * 0.7071067811865476
TAIL = (
    0.12411047596471954,
    0.12443560910041027,
    0.10865662380098591,
    0.10790671631036299,
    -0.010091621907114547,
    0.14834527631989725,
    -0.13897496529649409,
    0.03561197654899638,
)


def gelu_parts(h):
    t = 1.0 / (1.0 + TAIL_SCALE * jnp.abs(h))
    poly = TAIL[-1]
    for coefficient in TAIL[-2::-1]:
        poly = poly * t + coefficient
    bell = jnp.exp(-0.5 * h * h)
    tail = poly * t * bell
    phi = jnp.where(h < 0, tail, 1.0 - tail)
    return h * phi, phi + h * (bell * PHI_SCALE)


def up_kernel(npieces, table, count, att_ref, x_ref, small_ref, ub_ref, *rest):
    pieces = rest[:npieces]
    mid_ref, n2_ref, act_ref, gp_ref, w, sem = rest[npieces:]
    rb, width = x_ref.shape
    wide = act_ref.shape[1]

    @pl.when(pl.program_id(0) == 0)
    def _():
        copies = load_pieces(table, pieces, w, sem)
        for copy in copies:
            copy.start()
        for copy in copies:
            copy.wait()

    slot = lax.broadcasted_iota(jnp.int32, (rb, 1), 0) + pl.program_id(0) * rb
    valid = jnp.where(slot < count[0], 1.0, 0.0)
    branch = nn(att_ref[...], w[:, pl.ds(0, width)]) + small_ref[0:1, :]
    middle = x_ref[...] + valid * branch
    mid_ref[...] = middle
    xhat, _ = normalize(middle)
    n2 = (xhat * small_ref[1:2, :] + small_ref[2:3, :]).astype(BF16)
    n2_ref[...] = n2
    step = 512
    for c in range(wide // step):
        cut = pl.ds(c * step, step)
        hidden = nn(n2, w[:, pl.ds(width + c * step, step)]) + ub_ref[:, cut]
        act, slope = gelu_parts(hidden)
        act_ref[:, cut] = act.astype(BF16)
        gp_ref[:, cut] = slope.astype(BF16)


def up(table, count, att, x, small, ub, pieces, rb=256):
    total, width = x.shape
    wide = ub.shape[1]
    grid = (total // rb,)
    blk = lambda w: pl.BlockSpec((rb, w), lambda i: (i, 0))
    copies = piece_count(pieces)
    return pl.pallas_call(
        functools.partial(up_kernel, len(pieces)),
        grid=grid,
        in_specs=[SMEM, SMEM, blk(width), blk(width), whole(small.shape), whole((1, wide))] + [ANY] * len(pieces),
        out_specs=[blk(width), blk(width), blk(wide), blk(wide)],
        out_shape=[
            jax.ShapeDtypeStruct((total, width), F32),
            jax.ShapeDtypeStruct((total, width), BF16),
            jax.ShapeDtypeStruct((total, wide), BF16),
            jax.ShapeDtypeStruct((total, wide), BF16),
        ],
        scratch_shapes=[
            pltpu.VMEM((width, width + wide), BF16),
            pltpu.SemaphoreType.DMA((copies,)),
        ],
        compiler_params=params(grid),
        cost_estimate=cost(total * width * (width + wide) * 2, total * (width * 12 + wide * 4), total * wide * 2),
        name="up",
    )(table, count, att, x, small, ub, *pieces)


def down_kernel(nup, ndown, table, count, act_ref, gp_ref, mid_ref, cot_ref, gd_ref, small_ref, *rest):
    ups = rest[:nup]
    downs = rest[nup : nup + ndown]
    (out_ref, gm_ref, gb_ref, ga_ref, gu_ref, sums_ref, ubsum_ref, w, wd, sem, sem_d) = rest[nup + ndown :]
    i = pl.program_id(0)
    rb, width = mid_ref.shape
    wide = act_ref.shape[1]

    @pl.when(i == 0)
    def _():
        first = load_pieces(table, downs, wd, sem_d)
        second = load_pieces(table, ups, w, sem)
        for copy in first + second:
            copy.start()
        for copy in first + second:
            copy.wait()
        sums_ref[...] = jnp.zeros_like(sums_ref)
        ubsum_ref[...] = jnp.zeros_like(ubsum_ref)

    slot = lax.broadcasted_iota(jnp.int32, (rb, 1), 0) + i * rb
    valid = jnp.where(slot < count[0], 1.0, 0.0)
    middle = mid_ref[...]
    cot = cot_ref[...]
    gd = gd_ref[...]
    lowered = nn(act_ref[...], wd[...]) + small_ref[0:1, :]
    out_ref[...] = middle + valid * lowered
    step = 512
    gn2 = jnp.zeros((rb, width), F32)
    for c in range(wide // step):
        cut = pl.ds(c * step, step)
        g = nt(gd, wd[cut, :]) * gp_ref[:, cut].astype(F32)
        g_low = g.astype(BF16)
        gu_ref[:, cut] = g_low
        ubsum_ref[0:1, cut] += jnp.sum(g_low.astype(F32), axis=0, keepdims=True)
        gn2 = gn2 + nt(g_low, w[:, pl.ds(width + c * step, step)])
    xhat, inverse = normalize(middle)
    sums_ref[0:1, :] += jnp.sum(gn2 * xhat, axis=0, keepdims=True)
    sums_ref[1:2, :] += jnp.sum(gn2, axis=0, keepdims=True)
    e = gn2 * small_ref[1:2, :]
    back = (e - jnp.mean(e, axis=-1, keepdims=True) - xhat * jnp.mean(e * xhat, axis=-1, keepdims=True)) * inverse
    gmid = cot + back
    gm_ref[...] = gmid
    gb = (valid * gmid).astype(BF16)
    gb_ref[...] = gb
    sums_ref[2:3, :] += jnp.sum(gb.astype(F32), axis=0, keepdims=True)
    sums_ref[3:4, :] += jnp.sum(gd.astype(F32), axis=0, keepdims=True)
    ga_ref[...] = nt(gb, w[:, pl.ds(0, width)]).astype(BF16)


def down(table, count, act, gp, mid, cot, gd, small, ups, downs, rb=256):
    total, width = mid.shape
    wide = act.shape[1]
    grid = (total // rb,)
    blk = lambda w: pl.BlockSpec((rb, w), lambda i: (i, 0))
    return pl.pallas_call(
        functools.partial(down_kernel, len(ups), len(downs)),
        grid=grid,
        in_specs=[SMEM, SMEM, blk(wide), blk(wide), blk(width), blk(width), blk(width), whole(small.shape)]
        + [ANY] * (len(ups) + len(downs)),
        out_specs=[blk(width), blk(width), blk(width), blk(width), blk(wide), whole((8, width)), whole((8, wide))],
        out_shape=[
            jax.ShapeDtypeStruct((total, width), F32),
            jax.ShapeDtypeStruct((total, width), F32),
            jax.ShapeDtypeStruct((total, width), BF16),
            jax.ShapeDtypeStruct((total, width), BF16),
            jax.ShapeDtypeStruct((total, wide), BF16),
            jax.ShapeDtypeStruct((8, width), F32),
            jax.ShapeDtypeStruct((8, wide), F32),
        ],
        scratch_shapes=[
            pltpu.VMEM((width, width + wide), BF16),
            pltpu.VMEM((wide, width), BF16),
            pltpu.SemaphoreType.DMA((piece_count(ups),)),
            pltpu.SemaphoreType.DMA((piece_count(downs),)),
        ],
        compiler_params=params(grid),
        cost_estimate=cost(total * width * (width + 3 * wide) * 2, total * (width * 20 + wide * 6)),
        name="down",
    )(table, count, act, gp, mid, cot, gd, small, *ups, *downs)


def grad_kernel(nb, mids, reps, rows, cols_each, core, a_ref, *rest):
    b_refs = rest[:nb]
    keep_ref, send_ref = rest[nb:]
    part = core[0]
    a = a_ref[...]

    def spot(parity, mid, rep):
        return jnp.where(parity == 0, mid, rep), jnp.where(parity == 0, rep, mid)

    width = sum(b.shape[1] for b in b_refs)
    each = width // reps
    offset = 0
    for b_ref in b_refs:
        begin = 0
        while begin < b_ref.shape[1]:
            column = offset + begin
            step = min(b_ref.shape[1] - begin, each - column % each, cols_each)
            result = tn(a, b_ref[:, pl.ds(begin, step)])
            rep, cut = column // each, pl.ds(column % each, step)
            for pair in range(a.shape[1] // (2 * rows)):
                low = result[pair * 2 * rows : pair * 2 * rows + rows]
                high = result[pair * 2 * rows + rows : (pair + 1) * 2 * rows]
                zz, mid = pair // mids, pair % mids
                one, two = spot(part, mid, rep)
                keep_ref[one, two, zz, :, cut] = jnp.where(part == 0, low, high).astype(BF16)
                one, two = spot(1 - part, mid, rep)
                send_ref[one, two, zz, :, cut] = jnp.where(part == 0, high, low).astype(BF16)
            begin += step
        offset += b_ref.shape[1]


def weight_grad(core, a, bs, layout, name, block_of=None):
    slow, mids, reps = layout
    total, height = a.shape
    width = sum(w for _, w, _ in bs)
    rows = height // (slow * mids * 2)
    chunk = 384 if height % 384 == 0 and 384 % (2 * mids * rows) == 0 else 2 * mids * rows
    slows = chunk // (2 * mids * rows)
    grid = (height // chunk,)
    cols_each = min(width // reps, 768)
    out = jax.ShapeDtypeStruct((mids, reps, slow, rows, width // reps), BF16)
    spec = pl.BlockSpec((mids, reps, slows, rows, width // reps), lambda i: (0, 0, i, 0, 0))
    return pl.pallas_call(
        functools.partial(grad_kernel, len(bs), mids, reps, rows, cols_each),
        grid=grid,
        in_specs=[SMEM, pl.BlockSpec((total, chunk), lambda i: (0, i))]
        + [pl.BlockSpec((total, w), functools.partial(lambda at, i: (0, at), at)) for _, w, at in bs],
        out_specs=[spec, spec],
        out_shape=[out, out],
        compiler_params=params(grid),
        cost_estimate=cost(total * height * width * 2, total * (height + width) * 2 + height * width * 2),
        name=name,
    )(core, a, *[b for b, _, _ in bs])


def plain_grad_kernel(nb, a_ref, *rest):
    b_refs, out_ref = rest[:nb], rest[nb]
    a = a_ref[...]
    offset = 0
    for b_ref in b_refs:
        step = min(b_ref.shape[1], 768)
        for c in range(b_ref.shape[1] // step):
            out_ref[:, pl.ds(offset + c * step, step)] = tn(a, b_ref[:, pl.ds(c * step, step)])
        offset += b_ref.shape[1]


def plain_grad(a, bs, name):
    total, height = a.shape
    width = sum(w for _, w, _ in bs)
    chunk = 384
    grid = (height // chunk,)
    return pl.pallas_call(
        functools.partial(plain_grad_kernel, len(bs)),
        grid=grid,
        in_specs=[pl.BlockSpec((total, chunk), lambda i: (0, i))]
        + [pl.BlockSpec((total, w), functools.partial(lambda at, i: (0, at), at)) for _, w, at in bs],
        out_specs=pl.BlockSpec((chunk, width), lambda i: (i, 0)),
        out_shape=jax.ShapeDtypeStruct((height, width), F32),
        compiler_params=params(grid),
        cost_estimate=cost(total * height * width * 2, total * (height + width) * 2 + height * width * 4),
        name=name,
    )(a, *[b for b, _, _ in bs])


def unrotate(grad, cosine, sine):
    first, second = grad[:, :HALF], grad[:, HALF:]
    return first * cosine + second * sine, second * cosine - first * sine


def angle_grad(grad, rotated):
    return grad[:, HALF:] * rotated[:, :HALF] - grad[:, :HALF] * rotated[:, HALF:]


def back_kernel(g0, q_ref, k_ref, v_ref, do_ref, lse_ref, kb_ref, cos_ref, sin_ref, col_ref, row_ref,
                gq_ref, gk_ref, gv_ref, fsum_ref, bsum_ref, ds_s, p_s, dk_s, dv_s):
    g, r = pl.program_id(0), pl.program_id(1)
    rb, keys = q_ref.shape[0], k_ref.shape[0]
    here = pl.ds(pl.multiple_of(r * rb, rb), rb)
    q = q_ref[...]
    k = k_ref[...]
    v = v_ref[...]
    do = do_ref[...]
    zero = jnp.zeros_like(q)
    key = lax.broadcasted_iota(jnp.int32, (keys, rb), 0)
    query = lax.broadcasted_iota(jnp.int32, (keys, rb), 1) + r * rb
    mask = jnp.where(key == query, 0.0, jnp.broadcast_to(kb_ref[...], (keys, rb)))
    dq = jnp.zeros((rb, GW), F32)
    qms, doms = [], []
    for h in range(GH):
        qm = jnp.where(packed_head_mask(h), q, zero)
        dom = jnp.where(natural_head_mask(h), do, zero)
        qms.append(qm)
        doms.append(dom)
        soft = jnp.exp(nt(k, qm) + mask - lse_ref[h : h + 1, :])
        gp = nt(v, dom)
        inner = jnp.sum(soft * gp, axis=0, keepdims=True)
        ds = (soft * (gp - inner)).astype(BF16)
        cut = pl.ds(h * rb, rb)
        ds_s[:, cut] = ds
        p_s[:, cut] = soft.astype(BF16)
        km = jnp.where(packed_head_mask(h), k, jnp.zeros_like(k))
        dq = dq + tn(ds, km)
    dk = nn(ds_s[...], jnp.concatenate(qms, axis=0))
    dv = nn(p_s[...], jnp.concatenate(doms, axis=0))

    perm = group_perm(True)
    cosine, sine = cos_ref[here, :], sin_ref[here, :]
    dq = dq * (HD**-0.5)
    ang = angle_grad(dq, q.astype(F32) * (HD**0.5))
    first, second = unrotate(dq, cosine, sine)
    gq = nn(jnp.concatenate([first.astype(BF16), second.astype(BF16)], axis=1), perm)
    gq_ref[...] = gq.astype(BF16)
    col, row = col_ref[here, :], row_ref[here, :]
    fcol = jnp.sum(ang * col, axis=0, keepdims=True)
    frow = jnp.sum(ang * row, axis=0, keepdims=True)
    qsum = jnp.sum(gq, axis=0, keepdims=True)

    @pl.when(r == 0)
    def _():
        dk_s[...] = dk
        dv_s[...] = dv
        fsum_ref[0:1, :] = fcol
        fsum_ref[1:2, :] = frow
        bsum_ref[0:1, :] = qsum

    @pl.when(r > 0)
    def _():
        dk_s[...] += dk
        dv_s[...] += dv
        fsum_ref[0:1, :] += fcol
        fsum_ref[1:2, :] += frow
        bsum_ref[0:1, :] += qsum

    @pl.when(r == pl.num_programs(1) - 1)
    def _():
        dkf = dk_s[...]
        angk = angle_grad(dkf, k.astype(F32))
        fsum_ref[0:1, :] += jnp.sum(angk * col_ref[...], axis=0, keepdims=True)
        fsum_ref[1:2, :] += jnp.sum(angk * row_ref[...], axis=0, keepdims=True)
        one, two = unrotate(dkf, cos_ref[...], sin_ref[...])
        gk = nn(jnp.concatenate([one.astype(BF16), two.astype(BF16)], axis=1), perm)
        gk_ref[...] = gk.astype(BF16)
        bsum_ref[1:2, :] = jnp.sum(gk, axis=0, keepdims=True)
        gv = dv_s[...].astype(BF16)
        gv_ref[...] = gv
        bsum_ref[2:3, :] = jnp.sum(gv.astype(F32), axis=0, keepdims=True)


def attend_back(g0, l0, ng, q, k, v, do, lse, kb, cosine, sine, cols, rows, rb=256):
    total = q.shape[0]
    grid = (ng, total // rb)
    out = jax.ShapeDtypeStruct((total, ng * GW), BF16)
    rowblk = lambda g, r: (r, g + g0)
    colblk = lambda g, r: (0, g + g0)
    return pl.pallas_call(
        functools.partial(back_kernel, g0),
        grid=grid,
        in_specs=[
            pl.BlockSpec((rb, GW), lambda g, r: (r, g + l0)),
            pl.BlockSpec((total, GW), lambda g, r: (0, g + l0)),
            pl.BlockSpec((total, GW), lambda g, r: (0, g + l0)),
            pl.BlockSpec((rb, GW), rowblk),
            pl.BlockSpec((None, 8, rb), lambda g, r: (g + l0, 0, r)),
            whole((total, 1)),
            pl.BlockSpec((total, HALF), colblk),
            pl.BlockSpec((total, HALF), colblk),
            whole((total, 1)),
            whole((total, 1)),
        ],
        out_specs=[
            pl.BlockSpec((rb, GW), lambda g, r: (r, g)),
            pl.BlockSpec((total, GW), lambda g, r: (0, g)),
            pl.BlockSpec((total, GW), lambda g, r: (0, g)),
            pl.BlockSpec((None, 8, HALF), lambda g, r: (g, 0, 0)),
            pl.BlockSpec((None, 8, GW), lambda g, r: (g, 0, 0)),
        ],
        out_shape=[
            out,
            out,
            out,
            jax.ShapeDtypeStruct((ng, 8, HALF), F32),
            jax.ShapeDtypeStruct((ng, 8, GW), F32),
        ],
        scratch_shapes=[
            pltpu.VMEM((total, GH * rb), BF16),
            pltpu.VMEM((total, GH * rb), BF16),
            pltpu.VMEM((total, GW), F32),
            pltpu.VMEM((total, GW), F32),
        ],
        compiler_params=params(grid),
        cost_estimate=cost(total * total * GW * ng * 40, total * GW * ng * 16, total * total * GH * ng),
        name="attend_back",
    )(q, k, v, do, lse, kb, cosine, sine, cols, rows)


def final_kernel(grad_groups, counts, table, x_ref, gm_ref, gain_ref, *rest):
    grads, pieces, place = [], [], 0
    for groups in grad_groups:
        for g in range(groups):
            grads.append([rest[place + part][:, pl.ds(g * GW, GW)] for part in range(3)])
        place += 3
    for count in counts:
        pieces.append(rest[place : place + count])
        place += count
    out_ref, sums_ref = rest[place : place + 2]
    weights = rest[place + 2 : place + 2 + len(counts)]
    sems = rest[place + 2 + len(counts) :]

    @pl.when(pl.program_id(0) == 0)
    def _():
        copies = []
        for p, w, sem in zip(pieces, weights, sems):
            copies += load_pieces(table, p, w, sem)
        for copy in copies:
            copy.start()
        for copy in copies:
            copy.wait()
        sums_ref[...] = jnp.zeros_like(sums_ref)

    e = jnp.zeros(x_ref.shape, F32)
    group = 0
    for w in weights:
        for g in range(w.shape[1] // (3 * GW)):
            for part in range(3):
                e = e + nt(grads[group][part], w[:, pl.ds((g * 3 + part) * GW, GW)])
            group += 1
    xhat, inverse = normalize(x_ref[...])
    sums_ref[0:1, :] += jnp.sum(e * xhat, axis=0, keepdims=True)
    sums_ref[1:2, :] += jnp.sum(e, axis=0, keepdims=True)
    eg = e * gain_ref[...]
    back = (eg - jnp.mean(eg, axis=-1, keepdims=True) - xhat * jnp.mean(eg * xhat, axis=-1, keepdims=True)) * inverse
    out_ref[...] = gm_ref[...] + back


def final(table, x, gmid, gain, grad_sets, piece_sets, widths, rb=256):
    total, width = x.shape
    grid = (total // rb,)
    blk = lambda w: pl.BlockSpec((rb, w), lambda i: (i, 0))
    grads = [g for gs in grad_sets for g in gs]
    pieces = [p for ps in piece_sets for p in ps]
    return pl.pallas_call(
        functools.partial(final_kernel, [gs[0].shape[1] // GW for gs in grad_sets], [len(ps) for ps in piece_sets]),
        grid=grid,
        in_specs=[SMEM, blk(width), blk(width), whole((1, width))]
        + [blk(g.shape[1]) for g in grads]
        + [ANY] * len(pieces),
        out_specs=[blk(width), whole((8, width))],
        out_shape=[jax.ShapeDtypeStruct((total, width), F32), jax.ShapeDtypeStruct((8, width), F32)],
        scratch_shapes=[pltpu.VMEM((width, w), BF16) for w in widths]
        + [pltpu.SemaphoreType.DMA((piece_count(ps),)) for ps in piece_sets],
        compiler_params=params(grid),
        cost_estimate=cost(total * width * width * 6, total * width * 20 + width * width * 6),
        name="final",
    )(table, x, gmid, gain, *grads, *pieces)


def place():
    me = lax.axis_index("fsdp")
    return lax.axis_index("rep"), me // 4, (me // 2) % 2, me % 2


def move(value, step):
    moves = []
    for i in range(32):
        y, z, x, c = step(i // 16, (i // 4) % 4, (i // 2) % 2, i % 2)
        moves.append((i, y * 16 + z * 4 + x * 2 + c))
    return lax.ppermute(value, ("rep", "fsdp"), moves)


def across_core(value):
    return move(value, lambda y, z, x, c: (y, z, x, 1 - c))


def across_x(value):
    return move(value, lambda y, z, x, c: (y, z, 1 - x, c))


def across_rep(value):
    return move(value, lambda y, z, x, c: (1 - y, z, x, c))


def across_near(value):
    return move(value, lambda y, z, x, c: (y, z ^ 1, x, c))


def across_far(value):
    return move(value, lambda y, z, x, c: (y, z ^ 2, x, c))


def across_one(value):
    return move(value, lambda y, z, x, c: (y, z, 1 - x, c) if c == 0 else (1 - y, z, x, c))


def across_two(value):
    return move(value, lambda y, z, x, c: (1 - y, z, x, c) if c == 0 else (y, z, 1 - x, c))


def pick(array, index):
    return lax.dynamic_index_in_dim(array, index, 0, keepdims=False)


def pick_two(array, index):
    return lax.dynamic_slice_in_dim(array, 2 * index, 2, 0)


def own_half(shard):
    half = shard.shape[1] // 2
    return lax.dynamic_slice_in_dim(shard, lax.axis_index("rep") * half, half, 1)


def piece_table():
    y, z, x, c = place()
    slot = jnp.arange(4, dtype=jnp.int32)
    owners, halves = [], []

    def add(mid, core, half):
        owners.append((z ^ slot) * 4 + mid * 2 + core)
        halves.append(jnp.broadcast_to(half, (4,)))

    for core in (c, 1 - c):
        add(x, core, y)
        add(jnp.where(core == 0, x, 1 - x), core, jnp.where(core == 0, 1 - y, y))
        add(jnp.where(core == 0, 1 - x, x), core, jnp.where(core == 0, y, 1 - y))
        add(1 - x, core, 1 - y)
    return jnp.concatenate(owners + halves).astype(jnp.int32)


def gather_small(small):
    pair = jnp.stack([small, across_near(small)])
    column = jnp.concatenate([pair, across_far(pair)])
    both = jnp.stack([column, across_x(column)])
    every = jnp.stack([both, across_core(both)]).reshape(16, -1)
    _, z, x, c = place()
    slot = jnp.arange(16, dtype=jnp.int32)
    owner = (z ^ (slot & 3)) * 4 + (x ^ ((slot >> 2) & 1)) * 2 + (c ^ (slot >> 3))
    where = (slot[:, None] == owner[None, :]).astype(BF16)
    return jnp.dot(where, every, preferred_element_type=F32)


class Reduce:
    stages = (across_core, across_one, across_two, across_far, across_near, across_rep)

    def __init__(self, keep, send):
        self.keep, self.first, self.got, self.stage = keep, send, [], 0
        self.out = None

    def base(self, count, one, two=None, cut=None):
        step = lambda a, i: a if i is None else pick(a, i)
        total = None
        for source, used in ((self.keep, 0), (self.got[0], 0), *((g, n + 1) for n, g in enumerate(self.got[1:count]))):
            value = source
            if used < 1:
                value = step(value, one)
            if used < 2:
                value = step(value, two)
            if cut is not None:
                value = cut(value)
            value = value.astype(F32)
            total = value if total is None else total + value
        return total

    def level(self, index):
        return self.base(3, self.i1, self.i2, lambda a: pick(a, index)) + pick(self.got[3], index % 2).astype(F32)

    def send(self):
        y, z, x, c = place()
        self.i1, self.i2 = jnp.where(c == 0, x, y), jnp.where(c == 0, y, x)
        if self.stage == 0:
            return self.first
        if self.stage == 1:
            return self.base(1, 1 - self.i1).astype(BF16)
        if self.stage == 2:
            return self.base(2, self.i1, 1 - self.i2).astype(BF16)
        if self.stage == 3:
            return self.base(3, self.i1, self.i2, lambda a: pick_two(a, 1 - z // 2)).astype(BF16)
        if self.stage == 4:
            return self.level(z ^ 1).astype(BF16)
        self.total = self.level(z) + self.got[4].astype(F32)
        return self.total

    def take(self, value):
        self.stage += 1
        if self.stage == 6:
            y = lax.axis_index("rep")
            first = jnp.where(y == 0, self.total, value)
            second = jnp.where(y == 0, value, self.total)
            self.out = jnp.concatenate([first, second], axis=1)
        else:
            self.got.append(value)


class SmallReduce:
    stages = (across_core, across_x, across_far, across_near, across_rep)

    def __init__(self, rows):
        self.part, self.stage = rows.reshape(4, 2, 2, rows.shape[1]).transpose(2, 1, 0, 3), 0

    def send(self):
        y, z, x, c = place()
        if self.stage == 4:
            self.kept = self.part
            return self.part
        cut = pick_two if self.stage == 2 else pick
        index = (c, x, z // 2, z % 2)[self.stage]
        self.kept = cut(self.part, index)
        return cut(self.part, 1 - index)

    def take(self, value):
        self.stage += 1
        self.part = self.kept + value
        self.out = self.part


class Gather:
    stages = (across_near, across_far, across_two, across_one, across_core)

    def __init__(self, shard):
        self.part, self.stage, self.early = own_half(shard), 0, None

    def send(self):
        return self.part

    def take(self, value):
        self.stage += 1
        if self.stage == 1 or self.stage == 3:
            self.part = jnp.stack([self.part, value])
        elif self.stage == 2:
            self.part = jnp.concatenate([self.part, value])
        elif self.stage == 4:
            self.quad = jnp.stack([self.part, value]).reshape(4, *value.shape[1:])
            self.part = self.quad
        else:
            self.out = [self.quad, value]


def step(movers, kernel=None, *inputs):
    sends = [m.send() for m in movers]
    inputs, sends = lax.optimization_barrier((inputs, sends))
    got = [m.stages[m.stage](s) for m, s in zip(movers, sends)]
    outs = kernel(*inputs) if kernel is not None else ()
    outs, got = lax.optimization_barrier((outs, got))
    for m, g in zip(movers, got):
        m.take(g)
    return outs


def small_rows(parts, n):
    return jnp.concatenate([p.astype(F32).reshape(n, -1) for p in parts], axis=1)


def unpack(small_full, lengths, n):
    vectors = []
    offset = 0
    for length in lengths:
        vectors.append(small_full[:, offset : offset + length].reshape(1, n * length))
        offset += length
    return vectors


def group_columns(weight, g0, ng, width):
    cuts = []
    for g in range(g0, g0 + ng):
        cuts += [weight[:, part * width + g * GW : part * width + (g + 1) * GW] for part in range(3)]
    return jnp.concatenate(cuts, axis=1)


def local(tuned, n, tokens, pre_gain, pre_shift, inward_weight, inward_bias, rotary_freqs, outward_weight,
          outward_bias, mlp_gain, mlp_shift, up_weight, up_bias, down_weight, down_bias, keep_mask, kept_counts,
          patch_rows, patch_cols, cotangent):
    total, width = tokens.shape
    groups = width // GW
    wide = up_weight.shape[1]
    smalls = [pre_gain, pre_shift, inward_bias, rotary_freqs, outward_bias, mlp_gain, mlp_shift, up_bias, down_bias]
    lengths = [s.shape[0] for s in smalls]
    small = jnp.concatenate(smalls)[None, :]
    out_up = jnp.concatenate([outward_weight, up_weight], axis=1)
    splits = [(0, 1), (1, groups - 1)]
    inward_parts = [group_columns(inward_weight, g0, ng, width) for g0, ng in splits]

    slot = jnp.arange(total, dtype=jnp.int32)
    count = kept_counts
    valid = slot < count[0]
    key_bias = jnp.where(valid & (keep_mask[0] == 1), 0.0, NEG).astype(F32)
    rows_f = patch_rows.astype(F32).reshape(total, 1)
    cols_f = patch_cols.astype(F32).reshape(total, 1)
    gd = (valid.astype(F32)[:, None] * cotangent).astype(BF16)
    core = (lax.axis_index("fsdp") % 2).astype(jnp.int32)[None]

    if tuned:
        table = piece_table()
        first, second = Gather(inward_parts[0]), Gather(inward_parts[1])
        outup, downs = Gather(out_up), Gather(down_weight)
        small_full = gather_small(small)
        step([first, second])
        step([first])
        step([first, second])
        step([first, outup])
        step([first, second])
    else:
        gather = lambda a: lax.all_gather(a, "fsdp", axis=0, tiled=True)
        table = jnp.zeros((2,), jnp.int32)
        small_full = gather(small).astype(F32)

        class Whole:
            def __init__(self, shard):
                self.out = [gather(shard)[None, None]]

        first, second = Whole(inward_parts[0]), Whole(inward_parts[1])
        outup, downs = Whole(out_up), Whole(down_weight)

    def run(movers, kernel, *inputs):
        return step(movers, kernel, *inputs) if tuned else kernel(*inputs)

    f_gain, f_shift, f_bias, f_freqs, f_obias, f_mgain, f_mshift, f_ubias, f_dbias = unpack(small_full, lengths, n)
    pairs = f_freqs.reshape(-1, 2)
    fc, fr = pairs[:, 0][None, :], pairs[:, 1][None, :]
    small_up = jnp.concatenate([f_obias, f_mgain, f_mshift, jnp.zeros((5, width), F32)], axis=0)
    small_down = jnp.concatenate([f_dbias, f_mgain, jnp.zeros((6, width), F32)], axis=0)

    n1, cosine, sine = run([second], prologue, tokens, f_gain, f_shift, fc, fr, cols_f, rows_f)

    def attention(g0, ng):
        def both(*args):
            q, k, v = qkv(g0, ng, *args)
            return (q, k, v) + tuple(attend(q, k, v, key_bias[None, :]))
        return both

    q0, k0, v0, att0, lse0 = run([second, outup], attention(0, 1), table, n1, f_bias, cosine, sine, first.out)
    q1, k1, v1 = run([outup, downs], functools.partial(qkv, 1, groups - 1), table, n1, f_bias, cosine, sine, second.out)
    att1, lse1 = run([outup, downs], attend, q1, k1, v1, key_bias[None, :])
    if tuned:
        step([outup])
    att = jnp.concatenate([att0, att1], axis=1)
    middle, n2, act, slope = run([downs], up, table, count, att, tokens, small_up, f_ubias, outup.out)

    layout = (n // 4, 2, 2)

    def gradient(name, a, bs):
        if tuned:
            return weight_grad(core, a, [(b, b.shape[1], 0) for b in bs], layout, name)
        full = plain_grad(a, [(b, b.shape[1], 0) for b in bs], name)
        return lax.psum(lax.psum_scatter(full, "fsdp", scatter_dimension=0, tiled=True), "rep")

    class Done:
        def __init__(self, out):
            self.out = out

    def reduction(parts):
        return Reduce(*parts) if tuned else Done(parts)

    r_down = reduction(run([downs], functools.partial(gradient, "down_grad"), act, [gd]))
    if tuned:
        step([downs])
    outputs, gmid, gb, ga, gu, sums, ubsum = run(
        [r_down], down, table, count, act, slope, middle, cotangent, gd, small_down, outup.out, downs.out
    )
    r_up = reduction(run([r_down], functools.partial(gradient, "up_grad"), n2, [gu]))
    r_out = reduction(run([r_down, r_up], functools.partial(gradient, "out_grad"), att, [gb]))
    if tuned:
        step([r_out])
    backs = []
    heads = ((0, 0, q0, k0, v0, lse0), (1, 0, q1, k1, v1, lse1), (2, 1, q1, k1, v1, lse1))

    def back(movers, which):
        g0, l0, q, k, v, lse = heads[which]
        outs = run(movers, functools.partial(attend_back, g0, l0, 1), q, k, v, ga, lse, key_bias[:, None], cosine,
                   sine, cols_f, rows_f)
        backs.append(outs)

    def in_gradient(movers, name, which):
        bs = [backs[g][part] for g in which for part in range(3)]
        return reduction(run(movers, functools.partial(gradient, name), n1, bs))

    back([r_down, r_up, r_out], 0)
    back([r_down, r_up, r_out], 1)
    r_in0 = in_gradient([r_down], "in_grad0", (0, 1))
    if tuned:
        step([r_in0])
    back([r_up, r_out, r_in0], 2)
    r_in1 = in_gradient([r_up, r_out, r_in0], "in_grad1", (2,))
    if tuned:
        step([r_in1])
    grad_tokens, first_sums = run(
        [r_up, r_out, r_in0, r_in1], functools.partial(final, widths=[3 * GW, 6 * GW]),
        table, tokens, gmid, f_gain, [b[:3] for b in backs], [first.out, second.out]
    )
    fsum = jnp.concatenate([b[3] for b in backs], axis=0)
    bsum = jnp.concatenate([b[4] for b in backs], axis=0)
    d_freqs = jnp.stack([fsum[:, 0].reshape(-1), fsum[:, 1].reshape(-1)], axis=1).reshape(-1)
    small_grads = [
        bsum[:, :2].transpose(1, 0, 2),
        first_sums[0],
        first_sums[1],
        bsum[:, 2],
        d_freqs,
        sums[2],
        sums[0],
        sums[1],
        ubsum[0],
        sums[3],
    ]
    rows = small_rows(small_grads, n)
    if tuned:
        r_small = SmallReduce(rows)
        step([r_small, r_in0, r_in1])
        step([r_small, r_in0, r_in1])
        step([r_small, r_in1])
        step([r_small, r_in1])
        step([r_small])
        mine = r_small.out
    else:
        mine = lax.psum(lax.psum_scatter(rows, "fsdp", scatter_dimension=0, tiled=True), "rep")[0]
    pieces = []
    for r, ng in ((r_in0, 2), (r_in1, 1)):
        block = r.out.reshape(-1, ng, 3, GW)
        pieces += [block[:, g] for g in range(ng)]
    d_inward = jnp.stack(pieces, axis=2).reshape(-1, 3 * width)
    each = width // n
    cuts = []
    offset = 0
    for length in (2 * each, each, each, each, each, each, each, each, wide // n, each):
        cuts.append(lax.slice_in_dim(mine, offset, offset + length))
        offset += length
    o_bias, o_gain, o_shift, o_vbias, o_freqs, o_obias, o_mgain, o_mshift, o_ubias, o_dbias = cuts
    return (outputs, grad_tokens, o_gain, o_shift, d_inward, o_bias, o_vbias, o_freqs, r_out.out, o_obias,
            o_mgain, o_mshift, r_up.out, o_ubias, r_down.out, o_dbias)


def solution(mesh):
    n = mesh.shape["fsdp"]
    tuned = mesh.shape["rep"] == 2 and n == 16
    row = P(("rep", "fsdp"), None)
    vec, mat = P("fsdp"), P("fsdp", None)
    return jax.shard_map(
        functools.partial(local, tuned, n),
        mesh=mesh,
        in_specs=(row, vec, vec, mat, vec, vec, mat, vec, vec, vec, mat, vec, mat, vec, row,
                  P(("rep", "fsdp")), row, row, row),
        out_specs=(row, row, vec, vec, mat, vec, vec, vec, mat, vec, vec, vec, mat, vec, mat, vec),
        check_vma=False,
    )
```

time: 911 us -> 452 us (0.50)
  matrix products: 302 us -> 0.13 us
  Pallas kernels: 0 us -> 220 us
  waiting for transfers between devices: 244 us -> 54.5 us
  blocking collectives: 129 us -> 0 us
  starting transfers between devices: 0.36 us -> 53.5 us
  local copies, waits for them, and re-layouts: 83.9 us -> 46.2 us
  other arithmetic: 101 us -> 69.6 us
  loops' own time: 21.2 us -> 0 us
  between operations: 19.4 us -> 2.89 us
    dot_general x54 -> x1, matrix products: 302 us -> 0.13 us  [gather_small(): return jnp.dot(where, every, preferred_element_type=F32)]
    pallas_call x0 -> x16, Pallas kernels: none -> 220 us  [the longest x3 63.9 us: attend_back(): pl.pallas_call(functools.partial(back_kernel, g0), grid=grid, in_specs=[p...]
    reduce_scatter x4 -> x0, waiting for transfers between devices: 202 us -> none  [the longest x1 116 us: local(): lax.psum_scatter(grad_down_weight, 'fsdp', scatter_dimension=0, tiled=True)]
    unnamed x2 -> x0, blocking collectives: 123 us -> none
    ppermute x0 -> x59, waiting for transfers between devices: none -> 54.5 us  [move(): return lax.ppermute(value, ('rep', 'fsdp'), moves)]
    ppermute x0 -> x59, starting transfers between devices: none -> 53.5 us  [move(): return lax.ppermute(value, ('rep', 'fsdp'), moves)]
    reduce_sum x19 -> x0, other arithmetic: 50.7 us -> none  [the longest x6 14 us: attend_forward(): row_total = jnp.sum(exp_scores, axis=-1, keepdims=True)]
    psum x1 -> x0, waiting for transfers between devices: 39.6 us -> none  [local(): lax.psum((shards[0], shards[1], shards[2], shards[3], shards[4], shards[5...]
  transfers between devices with their start and end apart: 9 -> 59, of which waited for: 3 -> 18; matrix products, arithmetic and copies ran while one was open for 48% -> 12% of each run, Pallas kernels for 0% -> 49%
where the time goes in v1:
time: 452 us; the launch traced here: 447 us
  Pallas kernels  220 us (49%)
  other arithmetic  69.6 us (15%)
  waiting for transfers between devices  54.5 us (12%)
  starting transfers between devices  53.5 us (12%)
  local copies, waits for them, and re-layouts  46.2 us (10%)
    pallas_call x3, Pallas kernels, attend_back(): pl.pallas_call(functools.partial(back_kernel, g0), grid=grid, in_specs=[p...  63.9 us
    ppermute x59, waiting for transfers between devices, move(): return lax.ppermute(value, ('rep', 'fsdp'), moves)  54.5 us
    ppermute x59, starting transfers between devices, move(): return lax.ppermute(value, ('rep', 'fsdp'), moves)  53.5 us
    pallas_call x5, Pallas kernels, weight_grad(): pl.pallas_call(functools.partial(grad_kernel, len(bs), mids, reps, rows,...  35.2 us
    pallas_call x1, Pallas kernels, down(): pl.pallas_call(functools.partial(down_kernel, len(ups), len(downs)), grid...  30.5 us
    pallas_call x2, Pallas kernels, attend(): pl.pallas_call(attend_kernel, grid=grid, in_specs=[pl.BlockSpec((rb, GW),...  29.5 us
    pallas_call x1, Pallas kernels, up(): pl.pallas_call(functools.partial(up_kernel, len(pieces)), grid=grid, in_s...  26.2 us
    pallas_call x2, Pallas kernels, qkv(): pl.pallas_call(functools.partial(qkv_kernel, g0, len(pieces)), grid=grid,...  15.7 us
  transfers between devices with their start and end apart: 59, of which 18 were waited for; matrix products, arithmetic and copies ran while one was open for 12% of the time, Pallas kernels for 49%

profile of v1, /device:TPU:0, one launch (start us, length us, event | category | flops | bytes accessed | tf_op | source)
XLA Modules:
  0.0 446.8 jit_solution(11095597873093757054)
XLA Ops:
  5.3 3.1 collective-permute-start.5
  8.5 6.1 %concatenate.90 = bf16[672]{0:T(1024)(128)(2,1)S(1)} concatenate(bf16[48]{0:T(256)(128)(2,1)} %param.20, bf16[48]{0:T(256)(128)(2,1)} %param.21, bf16[144]{0:T(256)(128)(2,1)} %param.23, bf16[48]{0:T(256)(128)(2,1)} %param.24, bf16[48]{0:T(256)(128)(2,1)} %param.26, bf16[48]{0:T(256)(128)(2,1)} %param.27, bf16[48]{0:T(256)(128)(2,1)} %param.28, bf16[192]{0:T(256)(128)(2,1)} %param.30, ...), dimensions={0} | concatenate | bytes 2688 | tf_op jit(solution)/shard_map/concatenate | solution.py:939
  18.4 2.9 collective-permute-start.1
  21.5 5.1 %collective-permute-done.6 = bf16[2,48,384]{2,1,0:T(8,128)(2,1)S(1)} collective-permute-done((bf16[2,48,384]{2,1,0:T(8,128)(2,1)S(1)}, bf16[2,48,384]{2,1,0:T(8,128)(2,1)S(1)}, u32[]{:S(2)}, u32[]{:S(2)}) %collective-permute-start.6) | collective-permute-done | bytes 73760 | tf_op jit(solution)/shard_map/ppermute | solution.py:731
  31.8 4.0 collective-permute-done.8
  38.4 4.6 %collective-permute-done.10 = bf16[48,1920]{1,0:T(8,128)(2,1)S(1)} collective-permute-done((bf16[48,1920]{1,0:T(8,128)(2,1)S(1)}, bf16[48,1920]{1,0:T(8,128)(2,1)S(1)}, u32[]{:S(2)}, u32[]{:S(2)}) %collective-permute-start.10) | collective-permute-done | bytes 184352 | tf_op jit(solution)/shard_map/ppermute | solution.py:731
  47.3 2.8 collective-permute-done.12
  56.7 6.7 %prologue.1 = (bf16[1024,768]{1,0:T(8,128)(2,1)}, f32[1024,384]{1,0:T(8,128)}, f32[1024,384]{1,0:T(8,128)}) custom-call(f32[1024,768]{1,0:T(8,128)} %x_ref.2, f32[1,768]{1,0:T(1,128)} %reshape.432.gain_ref, f32[1,768]{1,0:T(1,128)} %reshape.433.shift_ref, f32[1,384]{1,0:T(1,128)} %broadcast_in_dim_squeeze.6.fc_ref, f32[1,384]{1,0:T(1,128)} %broadcast_in_dim_squeeze.7.fr_ref, ...), custom_call_target="tpu_custom_call" | custom-call | flops 31457280 | bytes 7864320 | tf_op jit(solution)/shard_map/prologue/pallas_call | solution.py:141
  67.5 7.0 %qkv.2 = (bf16[1024,256]{1,0:T(8,128)(2,1)}, bf16[1024,256]{1,0:T(8,128)(2,1)}, bf16[1024,256]{1,0:T(8,128)(2,1)}) custom-call(s32[64]{0:T(128)} %concatenate.89.table, bf16[1024,768]{1,0:T(8,128)(2,1)} %get-tuple-element.558.n1_ref.a_ref, f32[1,2304]{1,0:T(1,128)} %reshape.437.bias_ref, f32[1024,384]{1,0:T(8,128)} %get-tuple-element.540.cos_ref, ...), custom_call_target="tpu_custom_call" | custom-call | flops 1207959552 | bytes 7471104 | tf_op jit(solution)/shard_map/qkv/pallas_call | solution.py:205
  74.5 10.4 %attend.2 = (bf16[1024,256]{1,0:T(8,128)(2,1)}, f32[1,8,1024]{2,1,0:T(8,128)}) custom-call(bf16[1024,256]{1,0:T(8,128)(2,1)} %get-tuple-element.473.q_ref, bf16[1024,256]{1,0:T(8,128)(2,1)} %get-tuple-element.474.k_ref, bf16[1024,256]{1,0:T(8,128)(2,1)} %get-tuple-element.475.v_ref, f32[1,1024]{1,0:T(1,128)} %and_select_fusion.kb_ref), custom_call_target="tpu_custom_call" | custom-call | flops 4294967296 | bytes 2097152 | tf_op jit(solution)/shard_map/attend/pallas_call | solution.py:257
  84.9 2.8 collective-permute-done.15
  90.7 8.8 %qkv.3 = (bf16[1024,512]{1,0:T(8,128)(2,1)}, bf16[1024,512]{1,0:T(8,128)(2,1)}, bf16[1024,512]{1,0:T(8,128)(2,1)}) custom-call(s32[64]{0:T(128)} %concatenate.89.table, bf16[1024,768]{1,0:T(8,128)(2,1)} %get-tuple-element.558.n1_ref.a_ref, f32[1,2304]{1,0:T(1,128)} %reshape.437.bias_ref, f32[1024,384]{1,0:T(8,128)} %get-tuple-element.540.cos_ref, ...), custom_call_target="tpu_custom_call" | custom-call | flops 2415919104 | bytes 8650752 | tf_op jit(solution)/shard_map/qkv/pallas_call | solution.py:205
  101.6 3.1 fusion.54
  106.6 19.1 %attend.3 = (bf16[1024,512]{1,0:T(8,128)(2,1)}, f32[2,8,1024]{2,1,0:T(8,128)}) custom-call(bf16[1024,512]{1,0:T(8,128)(2,1)} %get-tuple-element.534.q_ref, bf16[1024,512]{1,0:T(8,128)(2,1)} %get-tuple-element.535.k_ref, bf16[1024,512]{1,0:T(8,128)(2,1)} %get-tuple-element.536.v_ref, f32[1,1024]{1,0:T(1,128)} %and_select_fusion.kb_ref), custom_call_target="tpu_custom_call" | custom-call | flops 8589934592 | bytes 4194304 | tf_op jit(solution)/shard_map/attend/pallas_call | solution.py:257
  137.8 26.2 %up.1 = (f32[1024,768]{1,0:T(8,128)}, bf16[1024,768]{1,0:T(8,128)(2,1)}, bf16[1024,3072]{1,0:T(8,128)(2,1)}, bf16[1024,3072]{1,0:T(8,128)(2,1)}) custom-call(s32[64]{0:T(128)} %concatenate.89.table, s32[1]{0:T(128)} %copy.91.count, bf16[1024,768]{1,0:T(8,128)(2,1)} %copy-done.25, f32[1024,768]{1,0:T(8,128)} %x_ref.2, f32[8,768]{1,0:T(8,128)} %get-tuple-element.403.small_ref, ...), custom_call_target="tpu_custom_call" | custom-call | flops 6039797760 | bytes 22020096 | tf_op jit(solution)/shard_map/up/pallas_call | solution.py:343
  167.6 10.3 %down_grad.1 = (bf16[2,2,4,192,384]{4,3,2,1,0:T(8,128)(2,1)}, bf16[2,2,4,192,384]{4,3,2,1,0:T(8,128)(2,1)}) custom-call(s32[1]{0:T(128)} %bitcast.34.core, bf16[1024,3072]{1,0:T(8,128)(2,1)} %get-tuple-element.425.a_ref.act_ref, bf16[1024,768]{1,0:T(8,128)(2,1)} %multiply_convert_fusion.rest_0_.gd_ref), custom_call_target="tpu_custom_call" | custom-call | flops 4831838208 | bytes 12582912 | tf_op jit(solution)/shard_map/down_grad/pallas_call | solution.py:487
  177.9 5.3 %collective-permute-done.22 = bf16[2,4,192,384]{3,2,1,0:T(8,128)(2,1)} collective-permute-done((bf16[2,4,192,384]{3,2,1,0:T(8,128)(2,1)}, bf16[2,4,192,384]{3,2,1,0:T(8,128)(2,1)}, u32[]{:S(2)}, u32[]{:S(2)}) %collective-permute-start.22) | collective-permute-done | bytes 1179680 | tf_op jit(solution)/shard_map/ppermute | solution.py:731
  186.5 4.5 %collective-permute-done.23.rest_3_ = bf16[4,4,192,384]{3,2,1,0:T(8,128)(2,1)S(1)} collective-permute-done((bf16[4,4,192,384]{3,2,1,0:T(8,128)(2,1)S(1)}, bf16[4,4,192,384]{3,2,1,0:T(8,128)(2,1)S(1)}, u32[]{:S(2)}, u32[]{:S(2)}) %collective-permute-start.23) | collective-permute-done | bytes 2359328 | tf_op jit(solution)/shard_map/ppermute | solution.py:731
  192.6 30.5 %down.1 = (f32[1024,768]{1,0:T(8,128)}, f32[1024,768]{1,0:T(8,128)}, bf16[1024,768]{1,0:T(8,128)(2,1)}, bf16[1024,768]{1,0:T(8,128)(2,1)}, bf16[1024,3072]{1,0:T...) custom-call(s32[64]{0:T(128)} %concatenate.89.table, s32[1]{0:T(128)} %copy.91.count, ...), custom_call_target="tpu_custom_call" | custom-call | flops 15703474176 | bytes 34603008 | tf_op jit(solution)/shard_map/down/pallas_call | solution.py:418
  223.1 2.9 fusion
  227.0 9.9 %up_grad.1 = (bf16[2,2,4,48,1536]{4,3,2,1,0:T(8,128)(2,1)}, bf16[2,2,4,48,1536]{4,3,2,1,0:T(8,128)(2,1)}) custom-call(s32[1]{0:T(128)} %bitcast.34.core, bf16[1024,768]{1,0:T(8,128)(2,1)} %get-tuple-element.454.a_ref, bf16[1024,3072]{1,0:T(8,128)(2,1)} %get-tuple-element.455.rest_0_), custom_call_target="tpu_custom_call" | custom-call | flops 4831838208 | bytes 12582912 | tf_op jit(solution)/shard_map/up_grad/pallas_call | solution.py:487
  236.9 5.7 %collective-permute-done.25 = bf16[2,4,192,384]{3,2,1,0:T(8,128)(2,1)} collective-permute-done((bf16[2,4,192,384]{3,2,1,0:T(8,128)(2,1)}, bf16[2,4,192,384]{3,2,1,0:T(8,128)(2,1)}, u32[]{:S(2)}, u32[]{:S(2)}) %collective-permute-start.25) | collective-permute-done | bytes 1179680 | tf_op jit(solution)/shard_map/ppermute | solution.py:731
  246.4 4.6 %out_grad.1 = (bf16[2,2,4,48,384]{4,3,2,1,0:T(8,128)(2,1)}, bf16[2,2,4,48,384]{4,3,2,1,0:T(8,128)(2,1)}) custom-call(s32[1]{0:T(128)} %bitcast.34.core, bf16[1024,768]{1,0:T(8,128)(2,1)} %copy-done.25, bf16[1024,768]{1,0:T(8,128)(2,1)} %get-tuple-element.463.rest_0_), custom_call_target="tpu_custom_call" | custom-call | flops 1207959552 | bytes 4325376 | tf_op jit(solution)/shard_map/out_grad/pallas_call | solution.py:487
  250.9 4.2 collective-permute-done.26
  258.1 3.0 fusion.1
  265.1 2.7 collective-permute-start.29
  268.7 21.2 %attend_back.3 = (bf16[1024,256]{1,0:T(8,128)(2,1)}, bf16[1024,256]{1,0:T(8,128)(2,1)}, bf16[1024,256]{1,0:T(8,128)(2,1)}, f32[1,8,128]{2,1,0:T(8,128)}, f32[1,8,256]{2,1,0:T(8,128)}) custom-call(bf16[1024,256]{1,0:T(8,128)(2,1)} %get-tuple-element.473.q_ref, bf16[1024,256]{1,0:T(8,128)(2,1)} %get-tuple-element.474.k_ref, ...), custom_call_target="tpu_custom_call" | custom-call | flops 10737418240 | bytes 4194304 | tf_op jit(solution)/shard_map/attend_back/pallas_call | solution.py:619
  300.6 21.3 %attend_back.4 = (bf16[1024,256]{1,0:T(8,128)(2,1)}, bf16[1024,256]{1,0:T(8,128)(2,1)}, bf16[1024,256]{1,0:T(8,128)(2,1)}, f32[1,8,128]{2,1,0:T(8,128)}, f32[1,8,256]{2,1,0:T(8,128)}) custom-call(bf16[1024,512]{1,0:T(8,128)(2,1)} %get-tuple-element.534.q_ref, bf16[1024,512]{1,0:T(8,128)(2,1)} %get-tuple-element.535.k_ref, ...), custom_call_target="tpu_custom_call" | custom-call | flops 10737418240 | bytes 4194304 | tf_op jit(solution)/shard_map/attend_back/pallas_call | solution.py:619
  325.9 6.0 %in_grad0.1 = (bf16[2,2,4,48,768]{4,3,2,1,0:T(8,128)(2,1)}, bf16[2,2,4,48,768]{4,3,2,1,0:T(8,128)(2,1)}) custom-call(s32[1]{0:T(128)} %bitcast.34.core, bf16[1024,768]{1,0:T(8,128)(2,1)} %get-tuple-element.558.n1_ref.a_ref, bf16[1024,256]{1,0:T(8,128)(2,1)} %get-tuple-element.576.rest_0_, bf16[1024,256]{1,0:T(8,128)(2,1)} %get-tuple-element.577.rest_1_, ...), custom_call_target="tpu_custom_call" | custom-call | flops 2415919104 | bytes 7077888 | tf_op jit(solution)/shard_map/in_grad0/pallas_call | solution.py:487
  348.0 21.4 %attend_back.5 = (bf16[1024,256]{1,0:T(8,128)(2,1)}, bf16[1024,256]{1,0:T(8,128)(2,1)}, bf16[1024,256]{1,0:T(8,128)(2,1)}, f32[1,8,128]{2,1,0:T(8,128)}, f32[1,8,256]{2,1,0:T(8,128)}) custom-call(bf16[1024,512]{1,0:T(8,128)(2,1)} %get-tuple-element.534.q_ref, bf16[1024,512]{1,0:T(8,128)(2,1)} %get-tuple-element.535.k_ref, ...), custom_call_target="tpu_custom_call" | custom-call | flops 10737418240 | bytes 4194304 | tf_op jit(solution)/shard_map/attend_back/pallas_call | solution.py:619
  379.2 4.5 %in_grad1.1 = (bf16[2,2,4,48,384]{4,3,2,1,0:T(8,128)(2,1)}, bf16[2,2,4,48,384]{4,3,2,1,0:T(8,128)(2,1)}) custom-call(s32[1]{0:T(128)} %bitcast.34.core, bf16[1024,768]{1,0:T(8,128)(2,1)} %get-tuple-element.558.n1_ref.a_ref, bf16[1024,256]{1,0:T(8,128)(2,1)} %get-tuple-element.582.rest_0_.rest_6_, bf16[1024,256]{1,0:T(8,128)(2,1)} %get-tuple-element.583.rest_1_.rest_7_, ...), custom_call_target="tpu_custom_call" | custom-call | flops 1207959552 | bytes 4325376 | tf_op jit(solution)/shard_map/in_grad1/pallas_call | solution.py:487
  396.3 12.2 %final.1 = (f32[1024,768]{1,0:T(8,128)}, f32[8,768]{1,0:T(8,128)}) custom-call(s32[64]{0:T(128)} %concatenate.89.table, f32[1024,768]{1,0:T(8,128)} %x_ref.2, f32[1024,768]{1,0:T(8,128)} %get-tuple-element.574.gm_ref, f32[1,768]{1,0:T(1,128)} %reshape.432.gain_ref, bf16[1024,256]{1,0:T(8,128)(2,1)} %get-tuple-element.576.rest_0_, ...), custom_call_target="tpu_custom_call" | custom-call | flops 3623878656 | bytes 19267584 | tf_op jit(solution)/shard_map/final/pallas_call | solution.py:705
  (366 shorter events, 161.2 us)
Async XLA Ops:
  5.3 16.0 %collective-permute-start.5 = (bf16[48,768]{1,0:T(8,128)(2,1)S(1)}, bf16[48,768]{1,0:T(8,128)(2,1)S(1)}, u32[]{:S(2)}, u32[]{:S(2)}) collective-permute-start(bf16[48,768]{1,0:T(8,128)(2,1)S(1)} %constant_dynamic-slice_fusion.9), channel_id=1, source_target_pairs={{0,4},{1,5},{2,6},{3,7},{4,0},{5,1},{6,2},{7,3},{8,12},{9,13},{10,... | collective-permute-start | bytes 221192 | tf_op jit(solution)/shard_map/ppermute | solution.py:731
  8.4 12.9 %collective-permute-start.4 = (bf16[48,384]{1,0:T(8,128)(2,1)S(1)}, bf16[48,384]{1,0:T(8,128)(2,1)S(1)}, u32[]{:S(2)}, u32[]{:S(2)}) collective-permute-start(bf16[48,384]{1,0:T(8,128)(2,1)S(1)} %fusion.34), channel_id=1, source_target_pairs={{0,4},{1,5},{2,6},{3,7},{4,0},{5,1},{6,2},{7,3},{8,12},{9,13},{10,... | collective-permute-start | bytes 110600 | tf_op jit(solution)/shard_map/ppermute | solution.py:731
  18.4 10.3 %collective-permute-start.1 = (bf16[2,1,672]{2,0,1:T(2,128)(2,1)S(1)}, bf16[2,1,672]{2,0,1:T(2,128)(2,1)S(1)}, u32[]{:S(2)}, u32[]{:S(2)}) collective-permute-start(bf16[2,1,672]{2,0,1:T(2,128)(2,1)S(1)} %pad_maximum_fusion.27), channel_id=1, source_target_pairs={{0,8},{1,9},{2,10},{3,11},{4,12},{5,13},{6,14},{7,15},{8,0},{9,1},... | collective-permute-start | bytes 8072 | tf_op jit(solution)/shard_map/ppermute | solution.py:731
  28.7 9.6 %collective-permute-start.2 = (bf16[4,1,672]{2,0,1:T(4,128)(2,1)S(1)}, bf16[4,1,672]{2,0,1:T(4,128)(2,1)S(1)}, u32[]{:S(2)}, u32[]{:S(2)}) collective-permute-start(bf16[4,1,672]{2,0,1:T(4,128)(2,1)S(1)} %pad_maximum_fusion.26), channel_id=1, source_target_pairs={{0,2},{1,3},{2,0},{3,1},{4,6},{5,7},{6,4},{7,5},{8,10},{9,11},{10,... | collective-permute-start | bytes 16136 | tf_op jit(solution)/shard_map/ppermute | solution.py:731
  51.2 12.1 %collective-permute-start.13 = (bf16[2,4,48,768]{3,2,1,0:T(8,128)(2,1)}, bf16[2,4,48,768]{3,2,1,0:T(8,128)(2,1)}, u32[]{:S(2)}, u32[]{:S(2)}) collective-permute-start(bf16[2,4,48,768]{3,2,1,0:T(8,128)(2,1)} %get-tuple-element.347), channel_id=1, source_target_pairs={{0,2},{1,17},{2,0},{3,19},{4,6},{5,21},{6,4},{7,23},{8,10},{9,25},... | collective-permute-start | bytes 1769480 | tf_op jit(solution)/shard_map/ppermute | solution.py:731
  65.6 22.1 %collective-permute-start.14 = (bf16[4,4,48,768]{3,2,1,0:T(8,128)(2,1)}, bf16[4,4,48,768]{3,2,1,0:T(8,128)(2,1)}, u32[]{:S(2)}, u32[]{:S(2)}) collective-permute-start(bf16[4,4,48,768]{3,2,1,0:T(8,128)(2,1)} %bitcast.20.rest_0_.rest_11_), channel_id=1, source_target_pairs={{0,1},{1,0},{2,3},{3,2},{4,5},{5,4},{6,7},{7,6},{8,9},{9,8},{10,11... | collective-permute-start | bytes 3538952 | tf_op jit(solution)/shard_map/ppermute | solution.py:731
  67.5 20.1 %collective-permute-start.15 = (bf16[2,48,1920]{2,1,0:T(8,128)(2,1)}, bf16[2,48,1920]{2,1,0:T(8,128)(2,1)}, u32[]{:S(2)}, u32[]{:S(2)}) collective-permute-start(bf16[2,48,1920]{2,1,0:T(8,128)(2,1)} %pad_maximum_fusion.12), channel_id=1, source_target_pairs={{0,8},{1,9},{2,10},{3,11},{4,12},{5,13},{6,14},{7,15},{8,0},{9,1},... | collective-permute-start | bytes 1105928 | tf_op jit(solution)/shard_map/ppermute | solution.py:731
  89.8 11.8 %collective-permute-start.16 = (bf16[4,48,1920]{2,1,0:T(8,128)(2,1)}, bf16[4,48,1920]{2,1,0:T(8,128)(2,1)}, u32[]{:S(2)}, u32[]{:S(2)}) collective-permute-start(bf16[4,48,1920]{2,1,0:T(8,128)(2,1)} %get-tuple-element.381), channel_id=1, source_target_pairs={{0,16},{1,3},{2,18},{3,1},{4,20},{5,7},{6,22},{7,5},{8,24},{9,11},... | collective-permute-start | bytes 2211848 | tf_op jit(solution)/shard_map/ppermute | solution.py:731
  105.5 20.3 %collective-permute-start.18 = (bf16[2,4,48,1920]{3,2,1,0:T(8,128)(2,1)}, bf16[2,4,48,1920]{3,2,1,0:T(8,128)(2,1)}, u32[]{:S(2)}, u32[]{:S(2)}) collective-permute-start(bf16[2,4,48,1920]{3,2,1,0:T(8,128)(2,1)} %get-tuple-element.394), channel_id=1, source_target_pairs={{0,2},{1,17},{2,0},{3,19},{4,6},{5,21},{6,4},{7,23},{8,10},{9,25},... | collective-permute-start | bytes 4423688 | tf_op jit(solution)/shard_map/ppermute | solution.py:731
  106.4 19.3 %collective-permute-start.19 = (bf16[2,192,384]{2,1,0:T(8,128)(2,1)}, bf16[2,192,384]{2,1,0:T(8,128)(2,1)S(1)}, u32[]{:S(2)}, u32[]{:S(2)}) collective-permute-start(bf16[2,192,384]{2,1,0:T(8,128)(2,1)} %pad_maximum_fusion.15), channel_id=1, source_target_pairs={{0,8},{1,9},{2,10},{3,11},{4,12},{5,13},{6,14},{7,15},{8,0},{9,1},... | collective-permute-start | bytes 884744 | tf_op jit(solution)/shard_map/ppermute | solution.py:731
  135.5 28.6 %collective-permute-start.21 = (bf16[4,192,384]{2,1,0:T(8,128)(2,1)}, bf16[4,192,384]{2,1,0:T(8,128)(2,1)}, u32[]{:S(2)}, u32[]{:S(2)}) collective-permute-start(bf16[4,192,384]{2,1,0:T(8,128)(2,1)} %get-tuple-element.411), channel_id=1, source_target_pairs={{0,16},{1,3},{2,18},{3,1},{4,20},{5,7},{6,22},{7,5},{8,24},{9,11},... | collective-permute-start | bytes 1769480 | tf_op jit(solution)/shard_map/ppermute | solution.py:731
  166.7 16.5 %collective-permute-start.22 = (bf16[2,4,192,384]{3,2,1,0:T(8,128)(2,1)}, bf16[2,4,192,384]{3,2,1,0:T(8,128)(2,1)}, u32[]{:S(2)}, u32[]{:S(2)}) collective-permute-start(bf16[2,4,192,384]{3,2,1,0:T(8,128)(2,1)} %get-tuple-element.420), channel_id=1, source_target_pairs={{0,2},{1,17},{2,0},{3,19},{4,6},{5,21},{6,4},{7,23},{8,10},{9,25},... | collective-permute-start | bytes 3538952 | tf_op jit(solution)/shard_map/ppermute | solution.py:731
  192.4 30.6 %collective-permute-start.24 = (bf16[2,2,4,192,384]{4,3,2,1,0:T(8,128)(2,1)}, bf16[2,2,4,192,384]{4,3,2,1,0:T(8,128)(2,1)}, u32[]{:S(2)}, u32[]{:S(2)}) collective-permute-start(bf16[2,2,4,192,384]{4,3,2,1,0:T(8,128)(2,1)} %get-tuple-element.442), channel_id=1, source_target_pairs={{0,1},{1,0},{2,3},{3,2},{4,5},{5,4},{6,7},{7,6},{8,9},{9,8},{10,11... | collective-permute-start | bytes 7077896 | tf_op jit(solution)/shard_map/ppermute | solution.py:731
  226.0 16.5 %collective-permute-start.25 = (bf16[2,4,192,384]{3,2,1,0:T(8,128)(2,1)}, bf16[2,4,192,384]{3,2,1,0:T(8,128)(2,1)}, u32[]{:S(2)}, u32[]{:S(2)}) collective-permute-start(bf16[2,4,192,384]{3,2,1,0:T(8,128)(2,1)} %fusion), channel_id=1, source_target_pairs={{0,2},{1,17},{2,0},{3,19},{4,6},{5,21},{6,4},{7,23},{8,10},{9,25},... | collective-permute-start | bytes 3538952 | tf_op jit(solution)/shard_map/ppermute | solution.py:731
  245.0 10.1 %collective-permute-start.27 = (bf16[2,2,4,48,1536]{4,3,2,1,0:T(8,128)(2,1)}, bf16[2,2,4,48,1536]{4,3,2,1,0:T(8,128)(2,1)}, u32[]{:S(2)}, u32[]{:S(2)}) collective-permute-start(bf16[2,2,4,48,1536]{4,3,2,1,0:T(8,128)(2,1)} %get-tuple-element.467), channel_id=1, source_target_pairs={{0,1},{1,0},{2,3},{3,2},{4,5},{5,4},{6,7},{7,6},{8,9},{9,8},{10,11... | collective-permute-start | bytes 7077896 | tf_op jit(solution)/shard_map/ppermute | solution.py:731
  245.0 10.1 %collective-permute-start.26 = (bf16[4,192,384]{2,1,0:T(8,128)(2,1)}, bf16[4,192,384]{2,1,0:T(8,128)(2,1)S(1)}, u32[]{:S(2)}, u32[]{:S(2)}) collective-permute-start(bf16[4,192,384]{2,1,0:T(8,128)(2,1)} %fusion.3), channel_id=1, source_target_pairs={{0,16},{1,3},{2,18},{3,1},{4,20},{5,7},{6,22},{7,5},{8,24},{9,11},... | collective-permute-start | bytes 1769480 | tf_op jit(solution)/shard_map/ppermute | solution.py:731
  262.0 28.0 %collective-permute-start.30 = (bf16[2,4,48,1536]{3,2,1,0:T(8,128)(2,1)}, bf16[2,4,48,1536]{3,2,1,0:T(8,128)(2,1)}, u32[]{:S(2)}, u32[]{:S(2)}) collective-permute-start(bf16[2,4,48,1536]{3,2,1,0:T(8,128)(2,1)} %fusion.1), channel_id=1, source_target_pairs={{0,2},{1,17},{2,0},{3,19},{4,6},{5,21},{6,4},{7,23},{8,10},{9,25},... | collective-permute-start | bytes 3538952 | tf_op jit(solution)/shard_map/ppermute | solution.py:731
  265.1 24.9 %collective-permute-start.29 = (bf16[2,192,384]{2,1,0:T(8,128)(2,1)}, bf16[2,192,384]{2,1,0:T(8,128)(2,1)}, u32[]{:S(2)}, u32[]{:S(2)}) collective-permute-start(bf16[2,192,384]{2,1,0:T(8,128)(2,1)} %fusion.9), channel_id=1, source_target_pairs={{0,8},{1,9},{2,10},{3,11},{4,12},{5,13},{6,14},{7,15},{8,0},{9,1},... | collective-permute-start | bytes 884744 | tf_op jit(solution)/shard_map/ppermute | solution.py:731
  267.8 22.2 %collective-permute-start.31 = (bf16[2,4,48,384]{3,2,1,0:T(8,128)(2,1)S(1)}, bf16[2,4,48,384]{3,2,1,0:T(8,128)(2,1)}, u32[]{:S(2)}, u32[]{:S(2)}) collective-permute-start(bf16[2,4,48,384]{3,2,1,0:T(8,128)(2,1)S(1)} %fusion.12), channel_id=1, source_target_pairs={{0,2},{1,17},{2,0},{3,19},{4,6},{5,21},{6,4},{7,23},{8,10},{9,25},... | collective-permute-start | bytes 884744 | tf_op jit(solution)/shard_map/ppermute | solution.py:731
  298.2 23.8 %collective-permute-start.33 = (bf16[4,48,1536]{2,1,0:T(8,128)(2,1)}, bf16[4,48,1536]{2,1,0:T(8,128)(2,1)}, u32[]{:S(2)}, u32[]{:S(2)}) collective-permute-start(bf16[4,48,1536]{2,1,0:T(8,128)(2,1)} %fusion.2), channel_id=1, source_target_pairs={{0,16},{1,3},{2,18},{3,1},{4,20},{5,7},{6,22},{7,5},{8,24},{9,11},... | collective-permute-start | bytes 1769480 | tf_op jit(solution)/shard_map/ppermute | solution.py:731
  299.4 22.5 %collective-permute-start.32 = (bf16[192,384]{1,0:T(8,128)(2,1)}, bf16[192,384]{1,0:T(8,128)(2,1)S(1)}, u32[]{:S(2)}, u32[]{:S(2)}) collective-permute-start(bf16[192,384]{1,0:T(8,128)(2,1)} %fusion.21), channel_id=1, source_target_pairs={{0,4},{1,5},{2,6},{3,7},{4,0},{5,1},{6,2},{7,3},{8,12},{9,13},{10,... | collective-permute-start | bytes 442376 | tf_op jit(solution)/shard_map/ppermute | solution.py:731
  299.4 22.5 %collective-permute-start.34 = (bf16[4,48,384]{2,1,0:T(8,128)(2,1)}, bf16[4,48,384]{2,1,0:T(8,128)(2,1)S(1)}, u32[]{:S(2)}, u32[]{:S(2)}) collective-permute-start(bf16[4,48,384]{2,1,0:T(8,128)(2,1)} %fusion.20), channel_id=1, source_target_pairs={{0,16},{1,3},{2,18},{3,1},{4,20},{5,7},{6,22},{7,5},{8,24},{9,11},... | collective-permute-start | bytes 442376 | tf_op jit(solution)/shard_map/ppermute | solution.py:731
  343.9 25.5 %collective-permute-start.39 = (bf16[2,4,48,768]{3,2,1,0:T(8,128)(2,1)}, bf16[2,4,48,768]{3,2,1,0:T(8,128)(2,1)}, u32[]{:S(2)}, u32[]{:S(2)}) collective-permute-start(bf16[2,4,48,768]{3,2,1,0:T(8,128)(2,1)} %fusion.4), channel_id=1, source_target_pairs={{0,2},{1,17},{2,0},{3,19},{4,6},{5,21},{6,4},{7,23},{8,10},{9,25},... | collective-permute-start | bytes 1769480 | tf_op jit(solution)/shard_map/ppermute | solution.py:731
  345.0 24.4 %collective-permute-start.37 = (bf16[2,48,1536]{2,1,0:T(8,128)(2,1)}, bf16[2,48,1536]{2,1,0:T(8,128)(2,1)S(1)}, u32[]{:S(2)}, u32[]{:S(2)}) collective-permute-start(bf16[2,48,1536]{2,1,0:T(8,128)(2,1)} %fusion.7), channel_id=1, source_target_pairs={{0,8},{1,9},{2,10},{3,11},{4,12},{5,13},{6,14},{7,15},{8,0},{9,1},... | collective-permute-start | bytes 884744 | tf_op jit(solution)/shard_map/ppermute | solution.py:731
  346.8 22.6 %collective-permute-start.38 = (bf16[2,48,384]{2,1,0:T(8,128)(2,1)}, bf16[2,48,384]{2,1,0:T(8,128)(2,1)S(1)}, u32[]{:S(2)}, u32[]{:S(2)}) collective-permute-start(bf16[2,48,384]{2,1,0:T(8,128)(2,1)} %fusion.28), channel_id=1, source_target_pairs={{0,8},{1,9},{2,10},{3,11},{4,12},{5,13},{6,14},{7,15},{8,0},{9,1},... | collective-permute-start | bytes 221192 | tf_op jit(solution)/shard_map/ppermute | solution.py:731
  374.8 12.0 %collective-permute-start.42 = (bf16[4,48,768]{2,1,0:T(8,128)(2,1)}, bf16[4,48,768]{2,1,0:T(8,128)(2,1)}, u32[]{:S(2)}, u32[]{:S(2)}) collective-permute-start(bf16[4,48,768]{2,1,0:T(8,128)(2,1)} %fusion.5), channel_id=1, source_target_pairs={{0,16},{1,3},{2,18},{3,1},{4,20},{5,7},{6,22},{7,5},{8,24},{9,11},... | collective-permute-start | bytes 884744 | tf_op jit(solution)/shard_map/ppermute | solution.py:731
  375.9 10.8 %collective-permute-start.40 = (bf16[48,1536]{1,0:T(8,128)(2,1)}, bf16[48,1536]{1,0:T(8,128)(2,1)}, u32[]{:S(2)}, u32[]{:S(2)}) collective-permute-start(bf16[48,1536]{1,0:T(8,128)(2,1)} %fusion.17), channel_id=1, source_target_pairs={{0,4},{1,5},{2,6},{3,7},{4,0},{5,1},{6,2},{7,3},{8,12},{9,13},{10,... | collective-permute-start | bytes 442376 | tf_op jit(solution)/shard_map/ppermute | solution.py:731
  377.7 9.1 %collective-permute-start.41 = (bf16[48,384]{1,0:T(8,128)(2,1)}, bf16[48,384]{1,0:T(8,128)(2,1)}, u32[]{:S(2)}, u32[]{:S(2)}) collective-permute-start(bf16[48,384]{1,0:T(8,128)(2,1)} %fusion.32), channel_id=1, source_target_pairs={{0,4},{1,5},{2,6},{3,7},{4,0},{5,1},{6,2},{7,3},{8,12},{9,13},{10,... | collective-permute-start | bytes 110600 | tf_op jit(solution)/shard_map/ppermute | solution.py:731
  391.9 16.7 %collective-permute-start.44 = (f32[48,1536]{1,0:T(8,128)S(1)}, f32[48,1536]{1,0:T(8,128)}, u32[]{:S(2)}, u32[]{:S(2)}) collective-permute-start(f32[48,1536]{1,0:T(8,128)S(1)} %fusion.18), channel_id=1, source_target_pairs={{0,16},{1,17},{2,18},{3,19},{4,20},{5,21},{6,22},{7,23},{8,24},{9,... | collective-permute-start | bytes 884744 | tf_op jit(solution)/shard_map/ppermute | solution.py:731
  392.9 15.8 %collective-permute-start.47 = (bf16[2,4,48,384]{3,2,1,0:T(8,128)(2,1)}, bf16[2,4,48,384]{3,2,1,0:T(8,128)(2,1)}, u32[]{:S(2)}, u32[]{:S(2)}) collective-permute-start(bf16[2,4,48,384]{3,2,1,0:T(8,128)(2,1)} %fusion.13), channel_id=1, source_target_pairs={{0,2},{1,17},{2,0},{3,19},{4,6},{5,21},{6,4},{7,23},{8,10},{9,25},... | collective-permute-start | bytes 884744 | tf_op jit(solution)/shard_map/ppermute | solution.py:731
  393.8 14.9 %collective-permute-start.46 = (bf16[2,48,768]{2,1,0:T(8,128)(2,1)}, bf16[2,48,768]{2,1,0:T(8,128)(2,1)}, u32[]{:S(2)}, u32[]{:S(2)}) collective-permute-start(bf16[2,48,768]{2,1,0:T(8,128)(2,1)} %fusion.16), channel_id=1, source_target_pairs={{0,8},{1,9},{2,10},{3,11},{4,12},{5,13},{6,14},{7,15},{8,0},{9,1},... | collective-permute-start | bytes 442376 | tf_op jit(solution)/shard_map/ppermute | solution.py:731
  395.5 13.1 %collective-permute-start.45 = (f32[48,384]{1,0:T(8,128)S(1)}, f32[48,384]{1,0:T(8,128)}, u32[]{:S(2)}, u32[]{:S(2)}) collective-permute-start(f32[48,384]{1,0:T(8,128)S(1)} %fusion.31), channel_id=1, source_target_pairs={{0,16},{1,17},{2,18},{3,19},{4,20},{5,21},{6,22},{7,23},{8,24},{9,... | collective-permute-start | bytes 221192 | tf_op jit(solution)/shard_map/ppermute | solution.py:731
  (75 other events, 551.6 us)
